TPU v7x, 32 devices: a whole 2x2x4 slice. The times are simulated.
32 devices in a mesh: cuts: 2 (over x), rows: 16 (over z, y, core).
Axes of the slice: x: 2, y: 2, z: 4, core: 2. Of those that a mesh axis runs over, the one named last changes fastest.
Arguments:
- start_modes: float32 [2, 64, 512, 128], P('cuts', 'rows'), may hold values from -6 to 6
- contrast: float32 [2, 64, 512], P('cuts', 'rows'), may hold values from 0 to 1
- rotations: float32 [2, 2, 128, 128], P('cuts'), may hold values from -0.2 to 1.2, as said below
- ordering: int32 [2, 2, 128], P('cuts'), may hold values from 0 to 127, each once within a row
Outputs:
- modes: float32 [2, 64, 512, 128], P('cuts', 'rows')
- coupling: float32 [2, 128, 128], P('cuts', 'rows')
- rayleigh: float32 [2, 128, 128], P('cuts', 'rows')
Inputs may be any that keep to these rules, and one draw needn't show every extreme that they name: `rotations`: each matrix is invertible.
All inputs are finite; a program needn't handle non-finite values.
Results may differ from a plain program's by a relative error of at most 0.00026.
Values sent between devices are 32-bit elements; how exact they have to be, the bound alone decides.
No kernel may reach another device: no remote copies, remote signals or barrier semaphores. Data moves between devices by JAX's collectives and lax.ppermute only.
A program may use at most 64 MiB of HBM per device.

v0:
```python
import functools

import jax
import jax.numpy as jnp
from jax import lax
from jax.experimental import pallas as pl
from jax.experimental.pallas import tpu as pltpu
from jax.sharding import PartitionSpec as P


DEGREE = 4
ITERS = 2
DEPTH = DEGREE * ITERS
LANES = 128
HIGHEST = lax.Precision.HIGHEST


def mm(a, b):
    return jnp.dot(a, b, precision=HIGHEST, preferred_element_type=jnp.float32)


def mm_t(a, b):
    return lax.dot_general(
        a, b, (((0,), (0,)), ((), ())), precision=HIGHEST, preferred_element_type=jnp.float32
    )


def spread(messages, dims, pos, col, at, sign, x, weight, cs):
    rows_here, wide = dims
    nm = x.shape[2]
    for i, message in enumerate(messages):
        for r in range(rows_here):
            x[pos[at + i] + sign * r, pl.ds(col, wide), :] = message[r * wide : (r + 1) * wide, :]
        cs[2 * rows_here * i : 2 * rows_here * (i + 1), :] = message[rows_here * wide :, :]
    turned = (1.6 * cs[...] - 0.4).T
    for i in range(len(messages)):
        for r in range(rows_here):
            row = pos[at + i] + sign * r
            c = 2 * (rows_here * i + r)
            weight[row, pl.ds(col, LANES), :] = jnp.broadcast_to(
                turned[:, c : c + 1], (LANES, nm)
            )
            weight[row, pl.ds(pl.multiple_of(col + LANES, 8), wide - LANES), :] = (
                jnp.broadcast_to(turned[: wide - LANES, c + 1 : c + 2], (wide - LANES, nm))
            )


def apply_rows(dst, src, weight, wide, sides, first, last, opening):
    left = DEPTH
    at_left, at_right = sides
    count = last - first
    strip = wide // 3 if wide % 24 == 0 else wide
    unroll = 4

    for c0 in range(left, left + wide, strip):
        c1 = c0 + strip

        def row(r, up, ctr, c0=c0, c1=c1):
            down = src[r + 1, c0:c1, :]
            s = (up + down) + (src[r, c0 - 1 : c1 - 1, :] + src[r, c0 + 1 : c1 + 1, :])
            v = weight[r, c0:c1, :] * ctr + 0.4 * s
            if opening:
                v = 0.5 * v
            else:
                v = v - dst[r, c0:c1, :]
            a, b = c0, c1
            if c0 == left:
                edge = v[:DEPTH]
                dst[r, a : a + DEPTH, :] = jnp.where(at_left == 1, jnp.zeros_like(edge), edge)
                v, a = v[DEPTH:], a + DEPTH
            if c1 == left + wide:
                edge = v[b - DEPTH - a :]
                dst[r, b - DEPTH : b, :] = jnp.where(at_right == 1, jnp.zeros_like(edge), edge)
                v, b = v[: b - DEPTH - a], b - DEPTH
            dst[r, a:b, :] = v
            return ctr, down

        def rows(i, pair):
            for j in range(unroll):
                pair = row(first + unroll * i + j, *pair)
            return pair

        pair = (src[first - 1, c0:c1, :], src[first, c0:c1, :])
        whole = count // unroll
        if whole > 1:
            pair = lax.fori_loop(0, whole, rows, pair)
        elif whole:
            pair = rows(0, pair)
        for r in range(first + whole * unroll, last):
            pair = row(r, *pair)


def halves(v):
    high = v.astype(jnp.bfloat16)
    low = (v - high.astype(jnp.float32)).astype(jnp.bfloat16)
    return jnp.concatenate([high, low], axis=1)


def fold(p):
    n, m = p.shape[0] // 2, p.shape[1] // 2
    return (p[:n, :m] + p[n:, m:]) + (p[:n, m:] + p[n:, :m])


def block_rows(buf, at, step, lanes_at, core):
    nm = buf.shape[2]

    def take(first, last):
        rows = buf[at + first * step : at + last * step, lanes_at : lanes_at + core, :]
        return halves(rows.reshape((last - first) * step * core, nm))

    return take


def add_gram(dst, a, b, first, last):
    left = a(first, last)
    right = left if b is a else b(first, last)
    dst[...] += fold(
        lax.dot_general(
            left, right, (((0,), (0,)), ((), ())), preferred_element_type=jnp.float32
        )
    )


def half_operator(x, weight, tmp, first, last, tall, core):
    nm = x.shape[2]
    c0, c1 = 2 * DEPTH, 2 * DEPTH + core

    def half(i, _):
        r = DEPTH + i
        ctr = x[r, c0:c1, :]
        spot = lax.broadcasted_iota(jnp.int32, (core, nm), 0)
        right = jnp.where(spot == core - 1, 0.0, x[r, c0 + 1 : c1 + 1, :])
        down = x[r + 1, c0:c1, :]
        down = jnp.where(i == tall - 1, jnp.zeros_like(down), down)
        tmp[i] = 0.25 * weight[r, c0:c1, :] * ctr + 0.2 * (right + down)
        return 0

    lax.fori_loop(first, last, half, 0)


def near_kernel(dims, pos, *refs):
    rows_here, group, wide, core = dims
    tall = rows_here * group
    known = tall + DEPTH
    n_near = group + group // 2
    at = 2 * group
    messages, refs = refs[:n_near], refs[n_near:]
    x, y, weight, start, gram1, gram2, ray, coup, cs, tmp = refs
    nm = x.shape[2]
    span = wide + 2 * DEPTH
    sign, col = pos[at], pl.multiple_of(pos[at + 1], 8)
    low, sides = pos[at + 2], (pos[at + 4], pos[at + 5])
    zero = jnp.zeros((2 * DEPTH, nm), jnp.float32)

    def clear(r, _):
        for buf in (x, y, weight):
            buf[r, 0 : 2 * DEPTH, :] = zero
            buf[r, span - 2 * DEPTH : span, :] = zero
        return 0

    lax.fori_loop(0, tall + 2 * DEPTH, clear, 0)
    blank = jnp.zeros((span, nm), jnp.float32)
    y[DEPTH - 1] = blank
    y[known] = blank
    spread(messages, (rows_here, wide), pos, col, 0, sign, x, weight, cs)
    for i in range(tall):
        start[i] = x[DEPTH + i, 2 * DEPTH : 2 * DEPTH + core, :]
    for total in (gram1, gram2, ray, coup):
        total[...] = jnp.zeros_like(total)
    take = block_rows(x, DEPTH, rows_here, 2 * DEPTH, core)
    for k in range(1, DEPTH + 1):
        dst, src = (y, x) if k % 2 else (x, y)
        opening = k % DEGREE == 1
        if k < DEPTH:

            @pl.when(low < DEPTH)
            def _(dst=dst, src=src, k=k, opening=opening):
                apply_rows(dst, src, weight, wide, sides, k, DEPTH, opening)

        apply_rows(dst, src, weight, wide, sides, DEPTH, known - k, opening)
        if k == DEGREE:
            add_gram(gram1, take, take, 0, group - DEGREE // rows_here)
    done = group // 2
    add_gram(gram2, take, take, 0, done)
    half_operator(x, weight, tmp, 0, (done - 1) * rows_here, tall, core)
    add_gram(ray, take, block_rows(tmp, 0, rows_here, 0, core), 0, done - 1)

    @pl.when(pos[at + 6] == 1)
    def _():
        add_gram(coup, take, block_rows(start, 0, rows_here, 0, core), 0, done)


def far_kernel(dims, pos, *refs):
    rows_here, group, wide, core = dims
    tall = rows_here * group
    known = tall + DEPTH
    n_far = group // 2
    at = 2 * group
    messages, refs = refs[:n_far], refs[n_far:]
    start, gram1_in, gram2_in, ray_in, coup_in, refs = *refs[3:8], refs[8:]
    x, y, weight, gram1, gram2, ray, coup, out, row0 = refs[:9]
    backs, cs, tmp = refs[9 : 8 + group], refs[8 + group], refs[9 + group]
    sign, col = pos[at], pl.multiple_of(pos[at + 1], 8)
    high, sides = pos[at + 3], (pos[at + 4], pos[at + 5])
    spread(messages, (rows_here, wide), pos, col, group + group // 2, sign, x, weight, cs)
    for total, before in ((gram1, gram1_in), (gram2, gram2_in), (ray, ray_in), (coup, coup_in)):
        total[...] = before[...]
    take = block_rows(x, DEPTH, rows_here, 2 * DEPTH, core)
    for k in range(1, DEPTH + 1):
        dst, src = (y, x) if k % 2 else (x, y)
        opening = k % DEGREE == 1
        apply_rows(dst, src, weight, wide, sides, known - k, known, opening)
        if k < DEPTH:

            @pl.when(high > known)
            def _(dst=dst, src=src, k=k, opening=opening):
                apply_rows(dst, src, weight, wide, sides, known, known + DEPTH - k, opening)

        if k == DEGREE:
            add_gram(gram1, take, take, group - DEGREE // rows_here, group)
    done = group // 2
    for i in range(tall):
        out[i] = x[DEPTH + i, 2 * DEPTH : 2 * DEPTH + core, :]
        for back in backs:
            at_end = rows_here * core + i
            back[at_end : at_end + 1, :] = x[DEPTH + i, 2 * DEPTH : 2 * DEPTH + 1, :]
    row0[...] = x[DEPTH, 2 * DEPTH : 2 * DEPTH + core, :]
    for k, back in enumerate(backs):
        for r in range(rows_here):
            back[r * core : (r + 1) * core, :] = x[
                DEPTH + pos[at + 7 + k] + r, 2 * DEPTH : 2 * DEPTH + core, :
            ]
    add_gram(gram2, take, take, done, group)
    half_operator(x, weight, tmp, (done - 1) * rows_here, tall, tall, core)
    add_gram(ray, take, block_rows(tmp, 0, rows_here, 0, core), done - 1, group)

    @pl.when(pos[at + 6] == 1)
    def _():
        add_gram(coup, take, block_rows(start, 0, rows_here, 0, core), done, group)


def late_kernel(dims, turn, out, recv, down, ray0, coup0, *refs):
    rows_here, tall, core = dims
    columns, (ray, coup, side) = refs[:-3], refs[-3:]
    coup[...] = coup0[...]
    add_gram(
        coup,
        block_rows(out, 0, rows_here, 0, core),
        block_rows(recv, 0, rows_here, 0, core),
        0,
        tall // rows_here,
    )
    for i in range(tall):
        total = jnp.zeros((1, side.shape[1]), jnp.float32)
        for k, column in enumerate(columns):
            there = column[pl.ds(rows_here * core + turn[0] + turn[1] * i, 1), :]
            total = jnp.where(turn[2 + k] == 1, there, total)
        side[i : i + 1, :] = total
    ray[...] = ray0[...] + 0.2 * (
        mm_t(out[tall - 1], down[...]) + mm_t(out[:, core - 1, :], side[...])
    )


def modes_kernel(dims, pos, *refs):
    rows_here, group, core = dims
    blocks, mix, modes = refs[:group], refs[group], refs[group + 1]
    nm = mix.shape[0]
    m = halves(mix[...])
    m = jnp.concatenate([m, m], axis=0)
    for k in range(group):
        at = pl.multiple_of(pos[3 * k] * core, core)
        for r in range(rows_here):
            row = pos[3 * k + 1] + pos[3 * k + 2] * r
            if k:
                v = blocks[k][pl.ds(pl.multiple_of(row * core, core), core), :]
            else:
                v = blocks[k][row]
            p = jnp.dot(halves(v), m, preferred_element_type=jnp.float32)
            modes[r, pl.ds(at, core), :] = p[:, :nm] + p[:, nm:]


SUB = 8


def inverse_factor(a, work, panel, w, big=32):
    n = a.shape[0]
    row_id = lax.broadcasted_iota(jnp.int32, (n, n), 0)
    col_id = lax.broadcasted_iota(jnp.int32, (n, n), 1)
    work[:, :n] = a
    work[:, n:] = (row_id == col_id).astype(jnp.float32)
    sub_id = lax.broadcasted_iota(jnp.int32, (SUB, n), 0)
    full = (SUB, n)
    for top in range(0, n, big):
        blocks = [
            [work[at : at + SUB, :n], work[at : at + SUB, n:]]
            for at in range(top, top + big, SUB)
        ]
        for j in range(big // SUB):
            at = top + j * SUB
            diag = blocks[j][0]
            e = {
                (i, k): jnp.broadcast_to(diag[i : i + 1, at + k : at + k + 1], full)
                for i in range(SUB)
                for k in range(i + 1)
            }
            low, inv = {}, []
            for k in range(SUB):
                inv.append(lax.rsqrt(e[k, k]))
                for i in range(k + 1, SUB):
                    low[i, k] = e[i, k] * inv[k]
                for m in range(k + 1, SUB):
                    for i in range(m, SUB):
                        e[i, m] = e[i, m] - low[i, k] * low[m, k]
            ups = []
            for k in range(SUB):
                row = [jnp.broadcast_to(part[k : k + 1, :], full) for part in blocks[j]]
                for m in range(k):
                    row = [p - low[k, m] * q for p, q in zip(row, ups[m])]
                ups.append([p * inv[k] for p in row])
            done = [ups[0][0], ups[0][1]]
            for k in range(1, SUB):
                done = [jnp.where(sub_id == k, p, q) for p, q in zip(ups[k], done)]
            blocks[j] = done
            for i in range(j + 1, big // SUB):
                cols = []
                for k in range(SUB):
                    c = jnp.broadcast_to(blocks[i][0][:, at + k : at + k + 1], full)
                    for m in range(k):
                        c = c - low[k, m] * cols[m]
                    cols.append(c * inv[k])
                for part in range(2):
                    for k in range(SUB):
                        blocks[i][part] = blocks[i][part] - cols[k] * ups[k][part]
        for j in range(big // SUB):
            at = top + j * SUB
            w[at : at + SUB, :] = blocks[j][1]
            panel[j * SUB : (j + 1) * SUB, :n] = blocks[j][0]
            panel[j * SUB : (j + 1) * SUB, n:] = blocks[j][1]
        if top + big < n:
            fix = mm_t(panel[:, :n], panel[...])
            work[top + big :, :] = work[top + big :, :] - fix[top + big :, :]


def mixing_kernel(scale, g1, g2, rot_at, order, mix, work, panel, w, rot, sem):
    fetch = pltpu.make_async_copy(rot_at, rot, sem)
    fetch.start()
    n = g1.shape[0]
    ids = lax.broadcasted_iota(jnp.int32, (n, n), 0)

    def turned(t):
        pick = (order[t : t + 1, :] == ids).astype(jnp.float32)
        return mm(rot[t], pick)

    inverse_factor(g1[...] * scale, work, panel, w)
    fetch.wait()
    m1 = mm_t(w[...], turned(0))
    inverse_factor(mm_t(m1, mm(g2[...] * scale, m1)), work, panel, w)
    m2 = mm_t(w[...], turned(1))
    mix[...] = mm(m1, m2)


def reversed_bits(value, count):
    out = 0
    while count > 1:
        out, value, count = 2 * out + value % 2, value // 2, count // 2
    return out


def project_kernel(peers, scale, first, ray, coup, before, mix, shares):
    nm = mix.shape[0]
    share = nm // peers
    m = mix[...] * scale

    def place(value, at):
        for r in range(peers):
            to = (2 * reversed_bits(r, peers) + at) * share
            shares[to : to + share, :] = value[r * share : (r + 1) * share, :]

    place(mm_t(mix[...], mm(ray[...] + ray[...].T, m)), 1)
    half = mm_t(coup[...], m)

    @pl.when(first[0] == 1)
    def _():
        place(half, 0)

    @pl.when(first[0] != 1)
    def _():
        place(mm_t(before[...], half), 0)


def scatter_sum(value, axis):
    peers = lax.axis_size(axis)
    me = lax.axis_index(axis)
    bit = 1
    while bit < peers:
        half = value.shape[0] // 2
        odd = (me & bit) != 0
        low, high = value[:half], value[half:]
        other = xor_swap(jnp.where(odd, low, high), axis, bit)
        value = jnp.where(odd, high, low) + other
        bit *= 2
    return value


def xor_swap(value, axis, bit):
    peers = lax.axis_size(axis)
    return lax.ppermute(value, axis, [(i, i ^ bit) for i in range(peers)])


def sum_pair(one, two, axis):
    peers = lax.axis_size(axis)
    odd = (lax.axis_index(axis) & 1) == 1
    mine, other, bit = jnp.where(odd, two, one), jnp.where(odd, one, two), 1
    while bit < peers:
        there = xor_swap(other, axis, bit)
        mine = mine + there
        other, bit = mine, 2 * bit
    other = xor_swap(mine, axis, 1)
    return jnp.where(odd, other, mine), jnp.where(odd, mine, other)


def body(start_modes, contrast, rotations, ordering):
    v0, section = start_modes[0], contrast[0]
    rows_here, columns, nm = v0.shape
    peers = lax.axis_size("rows")
    cuts = lax.axis_size("cuts")
    near = DEPTH // rows_here
    group = 2 * near
    core = columns // group
    wide = core + 2 * DEPTH
    tall = group * rows_here
    pixels = rows_here * peers * columns
    me = lax.axis_index("rows")
    cut = lax.axis_index("cuts")
    q = me % group
    block = me // group
    blocks = peers // group

    def window(k):
        at = jnp.clip((q ^ k) * core - DEPTH, 0, columns - wide)
        part = lax.dynamic_slice(v0, (0, at, 0), (rows_here, wide, nm)).reshape(-1, nm)
        tail = lax.dynamic_slice(section, (0, at), (rows_here, wide))
        tail = jnp.pad(tail, ((0, 0), (0, 2 * LANES - wide))).reshape(2 * rows_here, LANES)
        return jnp.concatenate([part, tail], axis=0)

    def hop(j, relayed=False):
        pairs = []
        for i in range(peers):
            z, s = i // group, i % group
            to = z + 1 if (s >= near) != relayed else z - 1
            if 0 <= to < blocks:
                pairs.append((i, to * group + (s ^ j)))
        return pairs

    windows = [window(k) for k in range(group)]
    arrived = [None] * group
    for k in reversed(range(1, group)):
        arrived[k] = xor_swap(windows[k], "rows", k)
    direct = [lax.ppermute(windows[j], "rows", hop(j)) for j in range(near)]
    relay = [lax.ppermute(arrived[k], "rows", hop(0, True)) for k in range(near, group)]
    messages = [windows[0]] + arrived[1:] + direct + relay

    lower = q >= near
    total = tall + 2 * DEPTH
    sign = jnp.where(lower, 1, -1)
    image = [DEPTH + (q ^ k) * rows_here for k in range(group)]
    for j in range(near):
        s = q ^ j
        image.append(jnp.where(lower, (s - near) * rows_here, DEPTH + tall + s * rows_here))
    for k in range(near, group):
        s = q ^ k
        image.append(jnp.where(lower, DEPTH + tall + s * rows_here, (s - near) * rows_here))
    at = jnp.clip(q * core - DEPTH, 0, columns - wide)
    top, bottom = block == 0, block == blocks - 1
    no_near = jnp.where(lower, top, bottom)
    no_far = jnp.where(lower, bottom, top)
    place = [jnp.where(lower, i, total - 1 - i) for i in image] + [
        sign,
        DEPTH + at - (q * core - DEPTH),
        jnp.where(no_near, DEPTH, 0),
        jnp.where(no_far, DEPTH + tall, total),
        q == 0,
        q == group - 1,
        cut == 0,
    ]
    for k in range(1, group):
        s = (q ^ k) * rows_here
        place.append(jnp.where(lower, s, tall - rows_here - s))
    place = jnp.stack([jnp.asarray(p, jnp.int32) for p in place])

    square = jax.ShapeDtypeStruct((nm, nm), jnp.float32)
    tile = jax.ShapeDtypeStruct((tall, core, nm), jnp.float32)
    span = wide + 2 * DEPTH
    field_buffer = jax.ShapeDtypeStruct((total, span, nm), jnp.float32)
    vmem = pl.BlockSpec(memory_space=pltpu.VMEM)
    smem = pl.BlockSpec(memory_space=pltpu.SMEM)
    params = pltpu.CompilerParams(vmem_limit_bytes=16 * 1024 * 1024)
    dims = (rows_here, group, wide, core)
    early, far = messages[: group + near], messages[group + near :]
    x, y, weight, start, *sums = pl.pallas_call(
        functools.partial(near_kernel, dims),
        out_shape=(field_buffer,) * 3 + (tile,) + (square,) * 4,
        in_specs=[smem] + [vmem] * len(early),
        out_specs=[vmem] * 8,
        scratch_shapes=[
            pltpu.VMEM((2 * rows_here * len(early), LANES), jnp.float32),
            pltpu.VMEM((tall, core, nm), jnp.float32),
        ],
        compiler_params=params,
        cost_estimate=pl.CostEstimate(flops=10**9, bytes_accessed=4 * 10**7, transcendentals=0),
        name="near",
    )(place, *early)
    n_far = len(far)
    back_block = jax.ShapeDtypeStruct((rows_here * core + tall, nm), jnp.float32)
    _, _, _, gram1, gram2, ray, coup, field, row0, *back = pl.pallas_call(
        functools.partial(far_kernel, dims),
        out_shape=(field_buffer,) * 3
        + (square,) * 4
        + (tile, jax.ShapeDtypeStruct((core, nm), jnp.float32))
        + (back_block,) * (group - 1),
        in_specs=[smem] + [vmem] * (n_far + 8),
        out_specs=[vmem] * (8 + group),
        input_output_aliases={1 + n_far + i: i for i in range(3)},
        scratch_shapes=[
            pltpu.VMEM((2 * rows_here * n_far, LANES), jnp.float32),
            pltpu.VMEM((tall, core, nm), jnp.float32),
        ],
        compiler_params=params,
        cost_estimate=pl.CostEstimate(flops=10**9, bytes_accessed=2 * 10**7, transcendentals=0),
        name="far",
    )(place, *far, x, y, weight, start, *sums)

    recv = lax.ppermute(field, "cuts", [(i, i + 1) for i in range(cuts - 1)])
    gram1, gram2 = sum_pair(gram1, gram2, "rows")
    down = lax.ppermute(row0, "rows", hop(0, True))
    sent = back
    back = []
    for k in range(1, group):
        back.append(xor_swap(sent[k - 1], "rows", k))

    big = min(nm, 32)
    mix = pl.pallas_call(
        functools.partial(mixing_kernel, 1.0 / pixels),
        out_shape=square,
        in_specs=[vmem, vmem, pl.BlockSpec(memory_space=pl.ANY), vmem],
        out_specs=vmem,
        compiler_params=params,
        cost_estimate=pl.CostEstimate(flops=10**9, bytes_accessed=4 * 10**7, transcendentals=0),
        scratch_shapes=[
            pltpu.VMEM((nm, 2 * nm), jnp.float32),
            pltpu.VMEM((big, 2 * nm), jnp.float32),
            pltpu.VMEM((nm, nm), jnp.float32),
            pltpu.VMEM(rotations.shape[1:], jnp.float32),
            pltpu.SemaphoreType.DMA,
        ],
        name="mixing",
    )(gram1, gram2, rotations[0], ordering[0])

    before = lax.ppermute(mix, "cuts", [(i, i + 1) for i in range(cuts - 1)])
    edges = [k for k in range(1, group) if k & (k + 1) == 0]
    beside = [back[k - 1] for k in edges]
    recv, down, beside, mix_now = lax.optimization_barrier((recv, down, beside, mix))
    turned = q == near - 1
    turn = [jnp.where(turned, tall - 1, 0), jnp.where(turned, -1, 1)]
    turn += [(((q ^ (q + 1)) == k) & (q != group - 1)).astype(jnp.int32) for k in edges]
    turn = jnp.stack(turn)
    ray, coup = pl.pallas_call(
        functools.partial(late_kernel, (rows_here, tall, core)),
        out_shape=(square, square),
        in_specs=[smem] + [vmem] * (5 + len(edges)),
        out_specs=[vmem] * 2,
        scratch_shapes=[pltpu.VMEM((tall, nm), jnp.float32)],
        compiler_params=params,
        cost_estimate=pl.CostEstimate(flops=10**9, bytes_accessed=10**7, transcendentals=0),
        name="late",
    )(turn.astype(jnp.int32), field, recv, down, ray, coup, *beside)
    share = nm // peers
    first = (cut == 0).astype(jnp.int32).reshape(1)
    shares = pl.pallas_call(
        functools.partial(project_kernel, peers, 1.0 / pixels),
        out_shape=jax.ShapeDtypeStruct((2 * nm, nm), jnp.float32),
        in_specs=[smem] + [vmem] * 4,
        out_specs=vmem,
        compiler_params=params,
        cost_estimate=pl.CostEstimate(flops=10**8, bytes_accessed=10**6, transcendentals=0),
        name="project",
    )(first, ray, coup, before, mix_now)
    shares = scatter_sum(shares, "rows")
    coupling, rayleigh = shares[:share], shares[share:]

    where = []
    for k in range(group):
        source = q ^ k
        base = 0
        if k == 0:
            base = jnp.where(lower, q * rows_here, tall - rows_here - q * rows_here)
        down_there = source >= near
        where += [
            source,
            jnp.where(down_there, base, base + rows_here - 1),
            jnp.where(down_there, 1, -1),
        ]
    where = jnp.stack([jnp.asarray(p, jnp.int32) for p in where])
    modes = pl.pallas_call(
        functools.partial(modes_kernel, (rows_here, group, core)),
        out_shape=jax.ShapeDtypeStruct((rows_here, columns, nm), jnp.float32),
        in_specs=[smem] + [vmem] * (group + 1),
        out_specs=vmem,
        compiler_params=params,
        cost_estimate=pl.CostEstimate(flops=10**9, bytes_accessed=10**7, transcendentals=0),
        name="modes",
    )(where, field, *back, mix)
    return modes[None], coupling[None], rayleigh[None]


def solution(mesh):
    placed = (
        P("cuts", "rows", None, None),
        P("cuts", "rows", None),
        P("cuts", None, None, None),
        P("cuts", None, None),
    )

    return jax.shard_map(
        body,
        mesh=mesh,
        in_specs=placed,
        out_specs=(P("cuts", "rows", None, None), P("cuts", "rows", None), P("cuts", "rows", None)),
        check_vma=False,
    )
```

profile of v0, /device:TPU:8, one launch (start us, length us, event | category | flops | bytes accessed | tf_op | source)
XLA Modules:
  0.0 89.5 jit_solution(11275935154936357095)
XLA Ops:
  1.6 1.4 %constant_dynamic-slice_fusion = (f32[1,4,144,128]{3,2,1,0:T(8,128)S(1)}, f32[1,4,144,128]{3,2,1,0:T(8,128)S(1)}, f32[1,4,144,128]{3,2,1,0:T(8,128)S(1)}, f32[1,4,144,128]{3,2,1,0:T(8,128)S(1)}) fusion(f32[1,4,512,128]{3,2,1,0:T(8,128)} %param.4, s32[]{:T(128)S(6)} %min.17, s32[]{:T(128)S(6)} %min.16, s32[]{:T(128)S(6)} %min.15, s32[]{:T(128)S(6)} %min.14), kind=kLoop, calls=%fused_computation.22 | loop fusion | bytes 2359312 | tf_op jit(solution)/shard_map/dynamic_slice | solution.py:441
  3.0 1.6 %collective-permute-start = (f32[584,128]{1,0:T(8,128)S(1)}, f32[584,128]{1,0:T(8,128)S(1)}, u32[]{:S(2)}, u32[]{:S(2)}) collective-permute-start(f32[584,128]{1,0:T(8,128)S(1)} %pad_maximum_fusion), channel_id=1, source_target_pairs={{0,2},{1,3},{2,0},{3,1},{4,6},{5,7},{6,4},{7,5},{8,10},{9,11},{10,... | collective-permute-start | bytes 897032 | tf_op jit(solution)/shard_map/ppermute | solution.py:407
  5.5 1.9 %collective-permute-start.5 = (f32[584,128]{1,0:T(8,128)S(1)}, f32[584,128]{1,0:T(8,128)S(1)}, u32[]{:S(2)}, u32[]{:S(2)}) collective-permute-start(f32[584,128]{1,0:T(8,128)S(1)} %pad_maximum_fusion.2.refs_0_), channel_id=1, source_target_pairs={{2,6},{3,7},{4,0},{5,1},{6,10},{7,11},{8,4},{9,5},{10,14},{11,15},... | collective-permute-start | bytes 897032 | tf_op jit(solution)/shard_map/ppermute | solution.py:459
  7.4 1.9 %collective-permute-start.6 = (f32[584,128]{1,0:T(8,128)S(1)}, f32[584,128]{1,0:T(8,128)S(1)}, u32[]{:S(2)}, u32[]{:S(2)}) collective-permute-start(f32[584,128]{1,0:T(8,128)S(1)} %pad_maximum_fusion.3), channel_id=1, source_target_pairs={{2,7},{3,6},{4,1},{5,0},{6,11},{7,10},{8,5},{9,4},{10,15},{11,14},... | collective-permute-start | bytes 897032 | tf_op jit(solution)/shard_map/ppermute | solution.py:459
  9.4 3.7 %collective-permute-done.refs_2_ = f32[584,128]{1,0:T(8,128)S(1)} collective-permute-done((f32[584,128]{1,0:T(8,128)S(1)}, f32[584,128]{1,0:T(8,128)S(1)}, u32[]{:S(2)}, u32[]{:S(2)}) %collective-permute-start) | collective-permute-done | bytes 299040 | tf_op jit(solution)/shard_map/ppermute | solution.py:407
  13.1 3.5 %collective-permute-start.1 = (f32[584,128]{1,0:T(8,128)S(1)}, f32[584,128]{1,0:T(8,128)S(1)}, u32[]{:S(2)}, u32[]{:S(2)}) collective-permute-start(f32[584,128]{1,0:T(8,128)S(1)} %collective-permute-done.refs_2_), channel_id=1, source_target_pairs={{0,4},{1,5},{4,8},{5,9},{6,2},{7,3},{8,12},{9,13},{10,6},{11,7},{1... | collective-permute-start | bytes 897032 | tf_op jit(solution)/shard_map/ppermute | solution.py:460
  17.4 3.5 %collective-permute-start.3 = (f32[584,128]{1,0:T(8,128)S(1)}, f32[584,128]{1,0:T(8,128)S(1)}, u32[]{:S(2)}, u32[]{:S(2)}) collective-permute-start(f32[584,128]{1,0:T(8,128)S(1)} %collective-permute-done.2.refs_3_), channel_id=1, source_target_pairs={{0,4},{1,5},{4,8},{5,9},{6,2},{7,3},{8,12},{9,13},{10,6},{11,7},{1... | collective-permute-start | bytes 897032 | tf_op jit(solution)/shard_map/ppermute | solution.py:460
  21.9 6.4 %near.1 = (f32[32,160,128]{2,1,0:T(8,128)S(1)}, f32[32,160,128]{2,1,0:T(8,128)S(1)}, f32[32,160,128]{2,1,0:T(8,128)S(1)}, f32[16,128,128]{2,1,0:T(8,128)S(1)}, f...) custom-call(s32[18]{0:T(128)S(1)} %stack.156.pos, ...), custom_call_target="tpu_custom_call" | custom-call | flops 1000000000 | bytes 40000000 | tf_op jit(solution)/shard_map/near/pallas_call | solution.py:500
  29.1 5.2 %far.1 = (f32[32,160,128]{2,1,0:T(8,128)S(1)}, f32[32,160,128]{2,1,0:T(8,128)S(1)}, f32[32,160,128]{2,1,0:T(8,128)S(1)}, f32[128,128]{1,0:T(8,128)S(1)}, f32[128...) custom-call(s32[18]{0:T(128)S(1)} %stack.156.pos, ...), custom_call_target="tpu_custom_call", output_to_operand_aliasing={{0}: (3, {}), {1}: (4, {}), {2}: (5, {})} | custom-call | flops 1000000000 | bytes 20000000 | tf_op jit(solution)/shard_map/far/pallas_call | solution.py:515
  34.3 3.1 %collective-permute-start.15 = (f32[16,128,128]{2,1,0:T(8,128)S(1)}, f32[16,128,128]{2,1,0:T(8,128)S(1)}, u32[]{:S(2)}, u32[]{:S(2)}) collective-permute-start(f32[16,128,128]{2,1,0:T(8,128)S(1)} %get-tuple-element.35.refs_0_.out), channel_id=1, source_target_pairs={{0,16},{1,17},{2,18},{3,19},{4,20},{5,21},{6,22},{7,23},{8,24},{9,... | collective-permute-start | bytes 3145736 | tf_op jit(solution)/shard_map/ppermute | solution.py:533
  38.7 2.4 %collective-permute-start.11 = (f32[128,128]{1,0:T(8,128)S(1)}, f32[128,128]{1,0:T(8,128)S(1)}, u32[]{:S(2)}, u32[]{:S(2)}) collective-permute-start(f32[128,128]{1,0:T(8,128)S(1)} %select_add_fusion.1), channel_id=1, source_target_pairs={{0,2},{1,3},{2,0},{3,1},{4,6},{5,7},{6,4},{7,5},{8,10},{9,11},{10,... | collective-permute-start | bytes 196616 | tf_op jit(solution)/shard_map/ppermute | solution.py:407
  41.1 2.4 %collective-permute-done.11 = f32[128,128]{1,0:T(8,128)S(1)} collective-permute-done((f32[128,128]{1,0:T(8,128)S(1)}, f32[128,128]{1,0:T(8,128)S(1)}, u32[]{:S(2)}, u32[]{:S(2)}) %collective-permute-start.11) | collective-permute-done | bytes 65568 | tf_op jit(solution)/shard_map/ppermute | solution.py:407
  44.1 3.8 %collective-permute-done.12 = f32[128,128]{1,0:T(8,128)S(1)} collective-permute-done((f32[128,128]{1,0:T(8,128)S(1)}, f32[128,128]{1,0:T(8,128)S(1)}, u32[]{:S(2)}, u32[]{:S(2)}) %collective-permute-start.12) | collective-permute-done | bytes 65568 | tf_op jit(solution)/shard_map/ppermute | solution.py:407
  47.9 2.1 %collective-permute-start.13 = (f32[128,128]{1,0:T(8,128)S(1)}, f32[128,128]{1,0:T(8,128)S(1)}, u32[]{:S(2)}, u32[]{:S(2)}) collective-permute-start(f32[128,128]{1,0:T(8,128)S(1)} %add.100), channel_id=1, source_target_pairs={{0,8},{1,9},{2,10},{3,11},{4,12},{5,13},{6,14},{7,15},{8,0},{9,1},... | collective-permute-start | bytes 196616 | tf_op jit(solution)/shard_map/ppermute | solution.py:407
  50.0 3.1 %collective-permute-done.13 = f32[128,128]{1,0:T(8,128)S(1)} collective-permute-done((f32[128,128]{1,0:T(8,128)S(1)}, f32[128,128]{1,0:T(8,128)S(1)}, u32[]{:S(2)}, u32[]{:S(2)}) %collective-permute-start.13) | collective-permute-done | bytes 65568 | tf_op jit(solution)/shard_map/ppermute | solution.py:407
  53.8 1.5 %collective-permute-start.9 = (f32[528,128]{1,0:T(8,128)S(1)}, f32[528,128]{1,0:T(8,128)S(1)}, u32[]{:S(2)}, u32[]{:S(2)}) collective-permute-start(f32[528,128]{1,0:T(8,128)S(1)} %get-tuple-element.38), channel_id=1, source_target_pairs={{0,3},{1,2},{2,1},{3,0},{4,7},{5,6},{6,5},{7,4},{8,11},{9,10},{10,... | collective-permute-start | bytes 811016 | tf_op jit(solution)/shard_map/ppermute | solution.py:407
  55.3 2.5 %collective-permute-start.16 = (f32[128,128]{1,0:T(8,128)}, f32[128,128]{1,0:T(8,128)S(1)}, u32[]{:S(2)}, u32[]{:S(2)}) collective-permute-start(f32[128,128]{1,0:T(8,128)} %copy-done.5), channel_id=1, source_target_pairs={{0,4},{1,5},{4,8},{5,9},{6,2},{7,3},{8,12},{9,13},{10,6},{11,7},{1... | collective-permute-start | bytes 196616 | tf_op jit(solution)/shard_map/ppermute | solution.py:535
  58.8 10.1 %mixing.1.refs_4_.mix = f32[128,128]{1,0:T(8,128)S(1)} custom-call(f32[128,128]{1,0:T(8,128)S(1)} %get-tuple-element.56.g1, f32[128,128]{1,0:T(8,128)S(1)} %get-tuple-element.55.g2, f32[2,128,128]{2,1,0:T(8,128)S(1)} %bitcast.52, s32[2,128]{1,0:T(2,128)S(1)} %bitcast.53), custom_call_target="tpu_custom_call" | custom-call | flops 1000000000 | bytes 40000000 | tf_op jit(solution)/shard_map/mixing/pallas_call | solution.py:542
  68.9 1.3 %collective-permute-start.17 = (f32[128,128]{1,0:T(8,128)S(1)}, f32[128,128]{1,0:T(8,128)S(1)}, u32[]{:S(2)}, u32[]{:S(2)}) collective-permute-start(f32[128,128]{1,0:T(8,128)S(1)} %mixing.1.refs_4_.mix), channel_id=1, source_target_pairs={{0,16},{1,17},{2,18},{3,19},{4,20},{5,21},{6,22},{7,23},{8,24},{9,... | collective-permute-start | bytes 196616 | tf_op jit(solution)/shard_map/ppermute | solution.py:559
  74.4 3.6 %collective-permute-done.19 = f32[64,128]{1,0:T(8,128)S(1)} collective-permute-done((f32[64,128]{1,0:T(8,128)S(1)}, f32[64,128]{1,0:T(8,128)S(1)}, u32[]{:S(2)}, u32[]{:S(2)}) %collective-permute-start.19) | collective-permute-done | bytes 32800 | tf_op jit(solution)/shard_map/ppermute | solution.py:407
  78.0 1.7 %collective-permute-start.20 = (f32[32,128]{1,0:T(8,128)S(1)}, f32[32,128]{1,0:T(8,128)S(1)}, u32[]{:S(2)}, u32[]{:S(2)}) collective-permute-start(f32[32,128]{1,0:T(8,128)S(1)} %slice_select_fusion.2), channel_id=1, source_target_pairs={{0,4},{1,5},{2,6},{3,7},{4,0},{5,1},{6,2},{7,3},{8,12},{9,13},{10,... | collective-permute-start | bytes 49160 | tf_op jit(solution)/shard_map/ppermute | solution.py:407
  79.8 2.0 %collective-permute-done.20 = f32[32,128]{1,0:T(8,128)S(1)} collective-permute-done((f32[32,128]{1,0:T(8,128)S(1)}, f32[32,128]{1,0:T(8,128)S(1)}, u32[]{:S(2)}, u32[]{:S(2)}) %collective-permute-start.20) | collective-permute-done | bytes 16416 | tf_op jit(solution)/shard_map/ppermute | solution.py:407
  82.6 4.3 %collective-permute-done.8.refs_2_ = f32[528,128]{1,0:T(8,128)S(1)} collective-permute-done((f32[528,128]{1,0:T(8,128)S(1)}, f32[528,128]{1,0:T(8,128)S(1)}, u32[]{:S(2)}, u32[]{:S(2)}) %collective-permute-start.8) | collective-permute-done | bytes 270368 | tf_op jit(solution)/shard_map/ppermute | solution.py:407
  86.9 2.0 %modes.1 = f32[4,512,128]{2,1,0:T(8,128)} custom-call(s32[12]{0:T(128)S(1)} %stack.135.pos, f32[16,128,128]{2,1,0:T(8,128)S(1)} %get-tuple-element.35.refs_0_.out, f32[528,128]{1,0:T(8,128)S(1)} %collective-permute-done.7.refs_1_.refs_0_, f32[528,128]{1,0:T(8,128)S(1)} %collective-permute-done.8.refs_2_, ...), custom_call_target="tpu_custom_call" | custom-call | flops 1000000000 | bytes 10000000 | tf_op jit(solution)/shard_map/modes/pallas_call | solution.py:604
  (72 shorter events, 13.5 us)
Async XLA Ops:
  3.0 10.0 %collective-permute-start = (f32[584,128]{1,0:T(8,128)S(1)}, f32[584,128]{1,0:T(8,128)S(1)}, u32[]{:S(2)}, u32[]{:S(2)}) collective-permute-start(f32[584,128]{1,0:T(8,128)S(1)} %pad_maximum_fusion), channel_id=1, source_target_pairs={{0,2},{1,3},{2,0},{3,1},{4,6},{5,7},{6,4},{7,5},{8,10},{9,11},{10,... | collective-permute-start | bytes 897032 | tf_op jit(solution)/shard_map/ppermute | solution.py:407
  4.7 12.7 %collective-permute-start.2 = (f32[584,128]{1,0:T(8,128)S(1)}, f32[584,128]{1,0:T(8,128)S(1)}, u32[]{:S(2)}, u32[]{:S(2)}) collective-permute-start(f32[584,128]{1,0:T(8,128)S(1)} %pad_maximum_fusion.1), channel_id=1, source_target_pairs={{0,3},{1,2},{2,1},{3,0},{4,7},{5,6},{6,5},{7,4},{8,11},{9,10},{10,... | collective-permute-start | bytes 897032 | tf_op jit(solution)/shard_map/ppermute | solution.py:407
  4.8 16.3 %collective-permute-start.4 = (f32[584,128]{1,0:T(8,128)S(1)}, f32[584,128]{1,0:T(8,128)S(1)}, u32[]{:S(2)}, u32[]{:S(2)}) collective-permute-start(f32[584,128]{1,0:T(8,128)S(1)} %pad_maximum_fusion.3), channel_id=1, source_target_pairs={{0,1},{1,0},{2,3},{3,2},{4,5},{5,4},{6,7},{7,6},{8,9},{9,8},{10,11... | collective-permute-start | bytes 897032 | tf_op jit(solution)/shard_map/ppermute | solution.py:407
  5.5 15.6 %collective-permute-start.5 = (f32[584,128]{1,0:T(8,128)S(1)}, f32[584,128]{1,0:T(8,128)S(1)}, u32[]{:S(2)}, u32[]{:S(2)}) collective-permute-start(f32[584,128]{1,0:T(8,128)S(1)} %pad_maximum_fusion.2.refs_0_), channel_id=1, source_target_pairs={{2,6},{3,7},{4,0},{5,1},{6,10},{7,11},{8,4},{9,5},{10,14},{11,15},... | collective-permute-start | bytes 897032 | tf_op jit(solution)/shard_map/ppermute | solution.py:459
  7.4 14.4 %collective-permute-start.6 = (f32[584,128]{1,0:T(8,128)S(1)}, f32[584,128]{1,0:T(8,128)S(1)}, u32[]{:S(2)}, u32[]{:S(2)}) collective-permute-start(f32[584,128]{1,0:T(8,128)S(1)} %pad_maximum_fusion.3), channel_id=1, source_target_pairs={{2,7},{3,6},{4,1},{5,0},{6,11},{7,10},{8,5},{9,4},{10,15},{11,14},... | collective-permute-start | bytes 897032 | tf_op jit(solution)/shard_map/ppermute | solution.py:459
  13.1 15.2 %collective-permute-start.1 = (f32[584,128]{1,0:T(8,128)S(1)}, f32[584,128]{1,0:T(8,128)S(1)}, u32[]{:S(2)}, u32[]{:S(2)}) collective-permute-start(f32[584,128]{1,0:T(8,128)S(1)} %collective-permute-done.refs_2_), channel_id=1, source_target_pairs={{0,4},{1,5},{4,8},{5,9},{6,2},{7,3},{8,12},{9,13},{10,6},{11,7},{1... | collective-permute-start | bytes 897032 | tf_op jit(solution)/shard_map/ppermute | solution.py:460
  17.4 11.7 %collective-permute-start.3 = (f32[584,128]{1,0:T(8,128)S(1)}, f32[584,128]{1,0:T(8,128)S(1)}, u32[]{:S(2)}, u32[]{:S(2)}) collective-permute-start(f32[584,128]{1,0:T(8,128)S(1)} %collective-permute-done.2.refs_3_), channel_id=1, source_target_pairs={{0,4},{1,5},{4,8},{5,9},{6,2},{7,3},{8,12},{9,13},{10,6},{11,7},{1... | collective-permute-start | bytes 897032 | tf_op jit(solution)/shard_map/ppermute | solution.py:460
  29.1 28.7 %copy-start.6 = (s32[1,2,128]{2,1,0:T(2,128)S(1)}, s32[1,2,128]{2,1,0:T(2,128)}, u32[]{:S(2)}) copy-start(s32[1,2,128]{2,1,0:T(2,128)} %param.7) | copy-start | bytes 3076
  34.3 36.0 %collective-permute-start.15 = (f32[16,128,128]{2,1,0:T(8,128)S(1)}, f32[16,128,128]{2,1,0:T(8,128)S(1)}, u32[]{:S(2)}, u32[]{:S(2)}) collective-permute-start(f32[16,128,128]{2,1,0:T(8,128)S(1)} %get-tuple-element.35.refs_0_.out), channel_id=1, source_target_pairs={{0,16},{1,17},{2,18},{3,19},{4,20},{5,21},{6,22},{7,23},{8,24},{9,... | collective-permute-start | bytes 3145736 | tf_op jit(solution)/shard_map/ppermute | solution.py:533
  37.4 1.3 %collective-permute-start.10 = (f32[128,128]{1,0:T(8,128)S(1)}, f32[128,128]{1,0:T(8,128)S(1)}, u32[]{:S(2)}, u32[]{:S(2)}) collective-permute-start(f32[128,128]{1,0:T(8,128)S(1)} %broadcast_select_fusion.2), channel_id=1, source_target_pairs={{0,1},{1,0},{2,3},{3,2},{4,5},{5,4},{6,7},{7,6},{8,9},{9,8},{10,11... | collective-permute-start | bytes 196616 | tf_op jit(solution)/shard_map/ppermute | solution.py:407
  38.7 4.8 %collective-permute-start.11 = (f32[128,128]{1,0:T(8,128)S(1)}, f32[128,128]{1,0:T(8,128)S(1)}, u32[]{:S(2)}, u32[]{:S(2)}) collective-permute-start(f32[128,128]{1,0:T(8,128)S(1)} %select_add_fusion.1), channel_id=1, source_target_pairs={{0,2},{1,3},{2,0},{3,1},{4,6},{5,7},{6,4},{7,5},{8,10},{9,11},{10,... | collective-permute-start | bytes 196616 | tf_op jit(solution)/shard_map/ppermute | solution.py:407
  41.1 29.1 %copy-start.2 = (f32[128,128]{1,0:T(8,128)S(1)}, f32[128,128]{1,0:T(8,128)}, u32[]{:S(2)}) copy-start(f32[128,128]{1,0:T(8,128)} %copy-done.1) | copy-start | bytes 196612
  43.5 4.3 %collective-permute-start.12 = (f32[128,128]{1,0:T(8,128)S(1)}, f32[128,128]{1,0:T(8,128)S(1)}, u32[]{:S(2)}, u32[]{:S(2)}) collective-permute-start(f32[128,128]{1,0:T(8,128)S(1)} %add.99), channel_id=1, source_target_pairs={{0,4},{1,5},{2,6},{3,7},{4,0},{5,1},{6,2},{7,3},{8,12},{9,13},{10,... | collective-permute-start | bytes 196616 | tf_op jit(solution)/shard_map/ppermute | solution.py:407
  47.9 5.2 %collective-permute-start.13 = (f32[128,128]{1,0:T(8,128)S(1)}, f32[128,128]{1,0:T(8,128)S(1)}, u32[]{:S(2)}, u32[]{:S(2)}) collective-permute-start(f32[128,128]{1,0:T(8,128)S(1)} %add.100), channel_id=1, source_target_pairs={{0,8},{1,9},{2,10},{3,11},{4,12},{5,13},{6,14},{7,15},{8,0},{9,1},... | collective-permute-start | bytes 196616 | tf_op jit(solution)/shard_map/ppermute | solution.py:407
  53.1 4.7 %collective-permute-start.14 = (f32[128,128]{1,0:T(8,128)S(1)}, f32[128,128]{1,0:T(8,128)S(1)}, u32[]{:S(2)}, u32[]{:S(2)}) collective-permute-start(f32[128,128]{1,0:T(8,128)S(1)} %add.101), channel_id=1, source_target_pairs={{0,1},{1,0},{2,3},{3,2},{4,5},{5,4},{6,7},{7,6},{8,9},{9,8},{10,11... | collective-permute-start | bytes 196616 | tf_op jit(solution)/shard_map/ppermute | solution.py:407
  53.3 16.9 %collective-permute-start.7 = (f32[528,128]{1,0:T(8,128)}, f32[528,128]{1,0:T(8,128)S(1)}, u32[]{:S(2)}, u32[]{:S(2)}) collective-permute-start(f32[528,128]{1,0:T(8,128)} %get-tuple-element.36), channel_id=1, source_target_pairs={{0,1},{1,0},{2,3},{3,2},{4,5},{5,4},{6,7},{7,6},{8,9},{9,8},{10,11... | collective-permute-start | bytes 811016 | tf_op jit(solution)/shard_map/ppermute | solution.py:407
  53.8 16.4 %collective-permute-start.9 = (f32[528,128]{1,0:T(8,128)S(1)}, f32[528,128]{1,0:T(8,128)S(1)}, u32[]{:S(2)}, u32[]{:S(2)}) collective-permute-start(f32[528,128]{1,0:T(8,128)S(1)} %get-tuple-element.38), channel_id=1, source_target_pairs={{0,3},{1,2},{2,1},{3,0},{4,7},{5,6},{6,5},{7,4},{8,11},{9,10},{10,... | collective-permute-start | bytes 811016 | tf_op jit(solution)/shard_map/ppermute | solution.py:407
  55.3 14.9 %collective-permute-start.16 = (f32[128,128]{1,0:T(8,128)}, f32[128,128]{1,0:T(8,128)S(1)}, u32[]{:S(2)}, u32[]{:S(2)}) collective-permute-start(f32[128,128]{1,0:T(8,128)} %copy-done.5), channel_id=1, source_target_pairs={{0,4},{1,5},{4,8},{5,9},{6,2},{7,3},{8,12},{9,13},{10,6},{11,7},{1... | collective-permute-start | bytes 196616 | tf_op jit(solution)/shard_map/ppermute | solution.py:535
  68.9 3.2 %collective-permute-start.17 = (f32[128,128]{1,0:T(8,128)S(1)}, f32[128,128]{1,0:T(8,128)S(1)}, u32[]{:S(2)}, u32[]{:S(2)}) collective-permute-start(f32[128,128]{1,0:T(8,128)S(1)} %mixing.1.refs_4_.mix), channel_id=1, source_target_pairs={{0,16},{1,17},{2,18},{3,19},{4,20},{5,21},{6,22},{7,23},{8,24},{9,... | collective-permute-start | bytes 196616 | tf_op jit(solution)/shard_map/ppermute | solution.py:559
  72.6 1.3 %collective-permute-start.18 = (f32[128,128]{1,0:T(8,128)S(1)}, f32[128,128]{1,0:T(8,128)S(1)}, u32[]{:S(2)}, u32[]{:S(2)}) collective-permute-start(f32[128,128]{1,0:T(8,128)S(1)} %slice_select_fusion), channel_id=1, source_target_pairs={{0,1},{1,0},{2,3},{3,2},{4,5},{5,4},{6,7},{7,6},{8,9},{9,8},{10,11... | collective-permute-start | bytes 196616 | tf_op jit(solution)/shard_map/ppermute | solution.py:407
  74.0 4.0 %collective-permute-start.19 = (f32[64,128]{1,0:T(8,128)S(1)}, f32[64,128]{1,0:T(8,128)S(1)}, u32[]{:S(2)}, u32[]{:S(2)}) collective-permute-start(f32[64,128]{1,0:T(8,128)S(1)} %slice_select_fusion.1), channel_id=1, source_target_pairs={{0,2},{1,3},{2,0},{3,1},{4,6},{5,7},{6,4},{7,5},{8,10},{9,11},{10,... | collective-permute-start | bytes 98312 | tf_op jit(solution)/shard_map/ppermute | solution.py:407
  78.0 3.8 %collective-permute-start.20 = (f32[32,128]{1,0:T(8,128)S(1)}, f32[32,128]{1,0:T(8,128)S(1)}, u32[]{:S(2)}, u32[]{:S(2)}) collective-permute-start(f32[32,128]{1,0:T(8,128)S(1)} %slice_select_fusion.2), channel_id=1, source_target_pairs={{0,4},{1,5},{2,6},{3,7},{4,0},{5,1},{6,2},{7,3},{8,12},{9,13},{10,... | collective-permute-start | bytes 49160 | tf_op jit(solution)/shard_map/ppermute | solution.py:407
  79.7 7.2 %collective-permute-start.8 = (f32[528,128]{1,0:T(8,128)S(1)}, f32[528,128]{1,0:T(8,128)S(1)}, u32[]{:S(2)}, u32[]{:S(2)}) collective-permute-start(f32[528,128]{1,0:T(8,128)S(1)} %get-tuple-element.37), channel_id=1, source_target_pairs={{0,2},{1,3},{2,0},{3,1},{4,6},{5,7},{6,4},{7,5},{8,10},{9,11},{10,... | collective-permute-start | bytes 811016 | tf_op jit(solution)/shard_map/ppermute | solution.py:407
  81.8 7.1 %collective-permute-start.21 = (f32[16,128]{1,0:T(8,128)S(1)}, f32[16,128]{1,0:T(8,128)S(1)}, u32[]{:S(2)}, u32[]{:S(2)}) collective-permute-start(f32[16,128]{1,0:T(8,128)S(1)} %slice_select_fusion.3), channel_id=1, source_target_pairs={{0,8},{1,9},{2,10},{3,11},{4,12},{5,13},{6,14},{7,15},{8,0},{9,1},... | collective-permute-start | bytes 24584 | tf_op jit(solution)/shard_map/ppermute | solution.py:407
  (5 other events, 48.2 us)
where the time goes:
time: 91.3 us; the launch traced here: 89.5 us
  starting transfers between devices  30.2 us (33%)
  waiting for transfers between devices  28.6 us (31%)
  Pallas kernels  25.3 us (28%)
  local copies, waits for them, and re-layouts  4.06 us (4%)
  between operations  1.14 us (1%)
    ppermute x15, waiting for transfers between devices, xor_swap(): return lax.ppermute(value, axis, [(i, i ^ bit) for i in range(peers)])  26.2 us
    ppermute x15, starting transfers between devices, xor_swap(): return lax.ppermute(value, axis, [(i, i ^ bit) for i in range(peers)])  12.5 us
    pallas_call x1, Pallas kernels, body(): pl.pallas_call(functools.partial(mixing_kernel, 1.0 / pixels), out_shape=...  10.1 us
    ppermute x2, starting transfers between devices, body(): lax.ppermute(arrived[k], 'rows', hop(0, True))  6.95 us
    pallas_call x1, Pallas kernels, body(): pl.pallas_call(functools.partial(near_kernel, dims), out_shape=(field_buf...  6.38 us
    pallas_call x1, Pallas kernels, body(): pl.pallas_call(functools.partial(far_kernel, dims), out_shape=(field_buff...  5.15 us
    ppermute x2, starting transfers between devices, body(): direct = [lax.ppermute(windows[j], 'rows', hop(j)) for j in range(near)]  3.84 us
    ppermute x1, starting transfers between devices, body(): recv = lax.ppermute(field, 'cuts', [(i, i + 1) for i in range(cuts - 1)])  3.08 us
  transfers between devices with their start and end apart: 22, of which 13 were waited for; matrix products, arithmetic and copies ran while one was open for 1% of the time, Pallas kernels for 22%

commit v1 on v0

--- a/solution.py
+++ b/solution.py
@@ -111,31 +111,40 @@
     return take
 
 
-def add_gram(dst, a, b, first, last):
-    left = a(first, last)
-    right = left if b is a else b(first, last)
-    dst[...] += fold(
-        lax.dot_general(
-            left, right, (((0,), (0,)), ((), ())), preferred_element_type=jnp.float32
-        )
+def add_gram(left, *pairs):
+    right = jnp.concatenate([r for _, r in pairs], axis=1)
+    p = lax.dot_general(
+        left, right, (((0,), (0,)), ((), ())), preferred_element_type=jnp.float32
     )
-
-
-def half_operator(x, weight, tmp, first, last, tall, core):
+    width = left.shape[1]
+    for i, (dst, _) in enumerate(pairs):
+        dst[...] += fold(p[:, i * width : (i + 1) * width])
+
+
+def half_operator(x, weight, tmp, first, last, core):
     nm = x.shape[2]
     c0, c1 = 2 * DEPTH, 2 * DEPTH + core
-
-    def half(i, _):
+    spot = lax.broadcasted_iota(jnp.int32, (DEPTH, nm), 0)
+    for i in range(first, last):
         r = DEPTH + i
-        ctr = x[r, c0:c1, :]
-        spot = lax.broadcasted_iota(jnp.int32, (core, nm), 0)
-        right = jnp.where(spot == core - 1, 0.0, x[r, c0 + 1 : c1 + 1, :])
-        down = x[r + 1, c0:c1, :]
-        down = jnp.where(i == tall - 1, jnp.zeros_like(down), down)
-        tmp[i] = 0.25 * weight[r, c0:c1, :] * ctr + 0.2 * (right + down)
-        return 0
-
-    lax.fori_loop(first, last, half, 0)
+        for a, b in ((c0, c1 - DEPTH), (c1 - DEPTH, c1)):
+            side = x[r, a + 1 : b + 1, :]
+            if b == c1:
+                side = jnp.where(spot == DEPTH - 1, 0.0, side)
+            if i:
+                side = side + x[r - 1, a:b, :]
+            tmp[i - first, a - c0 : b - c0, :] = (
+                0.25 * weight[r, a:b, :] * x[r, a:b, :] + 0.2 * side
+            )
+
+
+def finish_sums(x, weight, tmp, start, sums, first, last, core, opens):
+    gram, ray, coup = sums
+    field = block_rows(x, DEPTH, 1, 2 * DEPTH, core)(first, last)
+    half_operator(x, weight, tmp, first, last, core)
+    half = block_rows(tmp, 0, 1, 0, core)(0, last - first)
+    opening = block_rows(start, 0, 1, 0, core)(first, last)
+    add_gram(field, (gram, field), (ray, half), (coup, jnp.where(opens, opening, jnp.zeros_like(opening))))
 
 
 def near_kernel(dims, pos, *refs):
@@ -179,15 +188,9 @@
 
         apply_rows(dst, src, weight, wide, sides, DEPTH, known - k, opening)
         if k == DEGREE:
-            add_gram(gram1, take, take, 0, group - DEGREE // rows_here)
-    done = group // 2
-    add_gram(gram2, take, take, 0, done)
-    half_operator(x, weight, tmp, 0, (done - 1) * rows_here, tall, core)
-    add_gram(ray, take, block_rows(tmp, 0, rows_here, 0, core), 0, done - 1)
-
-    @pl.when(pos[at + 6] == 1)
-    def _():
-        add_gram(coup, take, block_rows(start, 0, rows_here, 0, core), 0, done)
+            f = take(0, group - DEGREE // rows_here)
+            add_gram(f, (gram1, f))
+    finish_sums(x, weight, tmp, start, (gram2, ray, coup), 0, tall // 2, core, pos[at + 6] == 1)
 
 
 def far_kernel(dims, pos, *refs):
@@ -198,8 +201,8 @@
     at = 2 * group
     messages, refs = refs[:n_far], refs[n_far:]
     start, gram1_in, gram2_in, ray_in, coup_in, refs = *refs[3:8], refs[8:]
-    x, y, weight, gram1, gram2, ray, coup, out, row0 = refs[:9]
-    backs, cs, tmp = refs[9 : 8 + group], refs[8 + group], refs[9 + group]
+    x, y, weight, packed, ray, coup, out, row0 = refs[:8]
+    backs, (cs, tmp, gram1, gram2) = refs[8 : 7 + group], refs[7 + group :]
     sign, col = pos[at], pl.multiple_of(pos[at + 1], 8)
     high, sides = pos[at + 3], (pos[at + 4], pos[at + 5])
     spread(messages, (rows_here, wide), pos, col, group + group // 2, sign, x, weight, cs)
@@ -217,26 +220,25 @@
                 apply_rows(dst, src, weight, wide, sides, known, known + DEPTH - k, opening)
 
         if k == DEGREE:
-            add_gram(gram1, take, take, group - DEGREE // rows_here, group)
-    done = group // 2
+            f = take(group - DEGREE // rows_here, group)
+            add_gram(f, (gram1, f))
     for i in range(tall):
         out[i] = x[DEPTH + i, 2 * DEPTH : 2 * DEPTH + core, :]
         for back in backs:
             at_end = rows_here * core + i
             back[at_end : at_end + 1, :] = x[DEPTH + i, 2 * DEPTH : 2 * DEPTH + 1, :]
-    row0[...] = x[DEPTH, 2 * DEPTH : 2 * DEPTH + core, :]
+    row0[...] = x[DEPTH + tall - 1, 2 * DEPTH : 2 * DEPTH + core, :]
     for k, back in enumerate(backs):
         for r in range(rows_here):
             back[r * core : (r + 1) * core, :] = x[
                 DEPTH + pos[at + 7 + k] + r, 2 * DEPTH : 2 * DEPTH + core, :
             ]
-    add_gram(gram2, take, take, done, group)
-    half_operator(x, weight, tmp, (done - 1) * rows_here, tall, tall, core)
-    add_gram(ray, take, block_rows(tmp, 0, rows_here, 0, core), done - 1, group)
-
-    @pl.when(pos[at + 6] == 1)
-    def _():
-        add_gram(coup, take, block_rows(start, 0, rows_here, 0, core), done, group)
+    finish_sums(x, weight, tmp, start, (gram2, ray, coup), tall // 2, tall, core, pos[at + 6] == 1)
+    half = gram1.shape[0] // 2
+    lane = lax.broadcasted_iota(jnp.int32, (half, 2 * half), 1)
+    packed[:half] = gram1[:half]
+    packed[half : 2 * half] = gram2[:half]
+    packed[2 * half :] = jnp.where(lane < half, pltpu.roll(gram2[half:], half, 1), gram1[half:])
 
 
 def late_kernel(dims, turn, out, recv, down, ray0, coup0, *refs):
@@ -244,11 +246,7 @@
     columns, (ray, coup, side) = refs[:-3], refs[-3:]
     coup[...] = coup0[...]
     add_gram(
-        coup,
-        block_rows(out, 0, rows_here, 0, core),
-        block_rows(recv, 0, rows_here, 0, core),
-        0,
-        tall // rows_here,
+        block_rows(out, 0, 1, 0, core)(0, tall), (coup, block_rows(recv, 0, 1, 0, core)(0, tall))
     )
     for i in range(tall):
         total = jnp.zeros((1, side.shape[1]), jnp.float32)
@@ -257,47 +255,47 @@
             total = jnp.where(turn[2 + k] == 1, there, total)
         side[i : i + 1, :] = total
     ray[...] = ray0[...] + 0.2 * (
-        mm_t(out[tall - 1], down[...]) + mm_t(out[:, core - 1, :], side[...])
+        mm_t(out[0], down[...]) + mm_t(out[:, core - 1, :], side[...])
     )
 
 
 def modes_kernel(dims, pos, *refs):
     rows_here, group, core = dims
-    blocks, mix, modes = refs[:group], refs[group], refs[group + 1]
+    blocks, (mix, modes, rows, sem) = refs[:group], refs[group:]
     nm = mix.shape[0]
     m = halves(mix[...])
     m = jnp.concatenate([m, m], axis=0)
-    for k in range(group):
-        at = pl.multiple_of(pos[3 * k] * core, core)
-        for r in range(rows_here):
+    copies = []
+    for r in range(rows_here):
+        for k in range(group):
+            at = pl.multiple_of(pos[3 * k] * core, core)
             row = pos[3 * k + 1] + pos[3 * k + 2] * r
             if k:
                 v = blocks[k][pl.ds(pl.multiple_of(row * core, core), core), :]
             else:
                 v = blocks[k][row]
             p = jnp.dot(halves(v), m, preferred_element_type=jnp.float32)
-            modes[r, pl.ds(at, core), :] = p[:, :nm] + p[:, nm:]
+            rows[r, pl.ds(at, core), :] = p[:, :nm] + p[:, nm:]
+        copies.append(pltpu.make_async_copy(rows.at[r], modes.at[r], sem.at[r]))
+        copies[-1].start()
+    for c in copies:
+        c.wait()
 
 
 SUB = 8
 
 
-def inverse_factor(a, work, panel, w, big=32):
-    n = a.shape[0]
-    row_id = lax.broadcasted_iota(jnp.int32, (n, n), 0)
-    col_id = lax.broadcasted_iota(jnp.int32, (n, n), 1)
-    work[:, :n] = a
-    work[:, n:] = (row_id == col_id).astype(jnp.float32)
-    sub_id = lax.broadcasted_iota(jnp.int32, (SUB, n), 0)
+def inverse_factor(a, work, panel):
+    n, big = a.shape[0], panel.shape[0]
+    work[...] = a
     full = (SUB, n)
+    lane = lax.broadcasted_iota(jnp.int32, full, 1)
+    sub = lax.broadcasted_iota(jnp.int32, full, 0)
     for top in range(0, n, big):
-        blocks = [
-            [work[at : at + SUB, :n], work[at : at + SUB, n:]]
-            for at in range(top, top + big, SUB)
-        ]
+        blocks = [work[at : at + SUB, :] for at in range(top, top + big, SUB)]
         for j in range(big // SUB):
             at = top + j * SUB
-            diag = blocks[j][0]
+            diag = blocks[j]
             e = {
                 (i, k): jnp.broadcast_to(diag[i : i + 1, at + k : at + k + 1], full)
                 for i in range(SUB)
@@ -311,51 +309,74 @@
                 for m in range(k + 1, SUB):
                     for i in range(m, SUB):
                         e[i, m] = e[i, m] - low[i, k] * low[m, k]
+            here = (lane >= at) & (lane < at + SUB)
+            unit = jnp.where(lane == at + sub, 1.0, 0.0)
+            diag = jnp.where(here, unit, diag)
             ups = []
             for k in range(SUB):
-                row = [jnp.broadcast_to(part[k : k + 1, :], full) for part in blocks[j]]
+                row = jnp.broadcast_to(diag[k : k + 1, :], full)
                 for m in range(k):
-                    row = [p - low[k, m] * q for p, q in zip(row, ups[m])]
-                ups.append([p * inv[k] for p in row])
-            done = [ups[0][0], ups[0][1]]
+                    row = row - low[k, m] * ups[m]
+                ups.append(row * inv[k])
+            done = ups[0]
             for k in range(1, SUB):
-                done = [jnp.where(sub_id == k, p, q) for p, q in zip(ups[k], done)]
+                done = jnp.where(sub == k, ups[k], done)
             blocks[j] = done
             for i in range(j + 1, big // SUB):
                 cols = []
                 for k in range(SUB):
-                    c = jnp.broadcast_to(blocks[i][0][:, at + k : at + k + 1], full)
+                    c = jnp.broadcast_to(blocks[i][:, at + k : at + k + 1], full)
                     for m in range(k):
                         c = c - low[k, m] * cols[m]
                     cols.append(c * inv[k])
-                for part in range(2):
-                    for k in range(SUB):
-                        blocks[i][part] = blocks[i][part] - cols[k] * ups[k][part]
+                rest = jnp.where(here, 0.0, blocks[i])
+                for k in range(SUB):
+                    rest = rest - cols[k] * ups[k]
+                blocks[i] = rest
         for j in range(big // SUB):
             at = top + j * SUB
-            w[at : at + SUB, :] = blocks[j][1]
-            panel[j * SUB : (j + 1) * SUB, :n] = blocks[j][0]
-            panel[j * SUB : (j + 1) * SUB, n:] = blocks[j][1]
+            work[at : at + SUB, :] = blocks[j]
+            panel[j * SUB : (j + 1) * SUB, :] = blocks[j]
         if top + big < n:
-            fix = mm_t(panel[:, :n], panel[...])
-            work[top + big :, :] = work[top + big :, :] - fix[top + big :, :]
-
-
-def mixing_kernel(scale, g1, g2, rot_at, order, mix, work, panel, w, rot, sem):
-    fetch = pltpu.make_async_copy(rot_at, rot, sem)
-    fetch.start()
-    n = g1.shape[0]
-    ids = lax.broadcasted_iota(jnp.int32, (n, n), 0)
-
-    def turned(t):
-        pick = (order[t : t + 1, :] == ids).astype(jnp.float32)
-        return mm(rot[t], pick)
-
-    inverse_factor(g1[...] * scale, work, panel, w)
-    fetch.wait()
-    m1 = mm_t(w[...], turned(0))
-    inverse_factor(mm_t(m1, mm(g2[...] * scale, m1)), work, panel, w)
-    m2 = mm_t(w[...], turned(1))
+            done = panel[...]
+            r = lax.broadcasted_iota(jnp.int32, done.shape, 0) + top
+            c = lax.broadcasted_iota(jnp.int32, done.shape, 1)
+            fix = mm_t(done, jnp.where((c > r) & (c < top + big), 0.0, done))
+            old = work[top + big :, :]
+            spot = lax.broadcasted_iota(jnp.int32, old.shape, 1)
+            old = jnp.where((spot >= top) & (spot < top + big), 0.0, old)
+            work[top + big :, :] = old - fix[top + big :, :]
+    row = lax.broadcasted_iota(jnp.int32, (n, n), 0)
+    column = lax.broadcasted_iota(jnp.int32, (n, n), 1)
+    work[...] = jnp.where(column <= row, work[...], 0.0)
+
+
+def turn_kernel(rot, order, turned):
+    nm = rot.shape[1]
+    ids = lax.broadcasted_iota(jnp.int32, (nm, nm), 0)
+    for t in range(rot.shape[0]):
+        turned[t] = mm(rot[t], (order[t : t + 1, :] == ids).astype(jnp.float32))
+
+
+def mixing_kernel(scale, packed, there, turned, mix, work, panel, gram):
+    n = mix.shape[0]
+    half = n // 2
+
+    def unpack(t):
+        at = t * half
+        upper = (packed[at : at + half, :] + there[at : at + half, :]) * scale
+        rest = (packed[2 * half :, :] + there[2 * half :, :]) * scale
+        if t:
+            rest = pltpu.roll(rest, half, 1)
+        gram[:half, :] = upper
+        gram[half:, :] = rest
+        gram[half:, :half] = upper.T[half:, :]
+        return gram[...]
+
+    inverse_factor(unpack(0), work, panel)
+    m1 = mm_t(work[...], turned[0])
+    inverse_factor(mm_t(m1, mm(unpack(1), m1)), work, panel)
+    m2 = mm_t(work[...], turned[1])
     mix[...] = mm(m1, m2)
 
 
@@ -407,16 +428,15 @@
     return lax.ppermute(value, axis, [(i, i ^ bit) for i in range(peers)])
 
 
-def sum_pair(one, two, axis):
+def sum_over(value, axis):
     peers = lax.axis_size(axis)
-    odd = (lax.axis_index(axis) & 1) == 1
-    mine, other, bit = jnp.where(odd, two, one), jnp.where(odd, one, two), 1
+    bit = 1
     while bit < peers:
-        there = xor_swap(other, axis, bit)
-        mine = mine + there
-        other, bit = mine, 2 * bit
-    other = xor_swap(mine, axis, 1)
-    return jnp.where(odd, other, mine), jnp.where(odd, mine, other)
+        there = xor_swap(value, axis, bit)
+        bit *= 2
+        if bit < peers:
+            value = value + there
+    return value, there
 
 
 def body(start_modes, contrast, rotations, ordering):
@@ -436,13 +456,6 @@
     block = me // group
     blocks = peers // group
 
-    def window(k):
-        at = jnp.clip((q ^ k) * core - DEPTH, 0, columns - wide)
-        part = lax.dynamic_slice(v0, (0, at, 0), (rows_here, wide, nm)).reshape(-1, nm)
-        tail = lax.dynamic_slice(section, (0, at), (rows_here, wide))
-        tail = jnp.pad(tail, ((0, 0), (0, 2 * LANES - wide))).reshape(2 * rows_here, LANES)
-        return jnp.concatenate([part, tail], axis=0)
-
     def hop(j, relayed=False):
         pairs = []
         for i in range(peers):
@@ -452,11 +465,23 @@
                 pairs.append((i, to * group + (s ^ j)))
         return pairs
 
+    def window(k):
+        at = jnp.clip((q ^ k) * core - DEPTH, 0, columns - wide)
+        part = lax.dynamic_slice(v0, (0, at, 0), (rows_here, wide, nm)).reshape(-1, nm)
+        tail = lax.dynamic_slice(section, (0, at), (rows_here, wide))
+        tail = jnp.pad(tail, ((0, 0), (0, 2 * LANES - wide))).reshape(2 * rows_here, LANES)
+        return jnp.concatenate([part, tail], axis=0)
+
+    vmem = pl.BlockSpec(memory_space=pltpu.VMEM)
+    smem = pl.BlockSpec(memory_space=pltpu.SMEM)
+    hbm = pl.BlockSpec(memory_space=pltpu.HBM)
     windows = [window(k) for k in range(group)]
     arrived = [None] * group
     for k in reversed(range(1, group)):
         arrived[k] = xor_swap(windows[k], "rows", k)
-    direct = [lax.ppermute(windows[j], "rows", hop(j)) for j in range(near)]
+    direct = []
+    for j in range(near):
+        direct.append(lax.ppermute(windows[j], "rows", hop(j)))
     relay = [lax.ppermute(arrived[k], "rows", hop(0, True)) for k in range(near, group)]
     messages = [windows[0]] + arrived[1:] + direct + relay
 
@@ -492,19 +517,23 @@
     tile = jax.ShapeDtypeStruct((tall, core, nm), jnp.float32)
     span = wide + 2 * DEPTH
     field_buffer = jax.ShapeDtypeStruct((total, span, nm), jnp.float32)
-    vmem = pl.BlockSpec(memory_space=pltpu.VMEM)
-    smem = pl.BlockSpec(memory_space=pltpu.SMEM)
-    params = pltpu.CompilerParams(vmem_limit_bytes=16 * 1024 * 1024)
+
+    def grant(mib):
+        return pltpu.CompilerParams(vmem_limit_bytes=mib * 1024 * 1024)
+
+    params = grant(10)
     dims = (rows_here, group, wide, core)
     early, far = messages[: group + near], messages[group + near :]
     x, y, weight, start, *sums = pl.pallas_call(
         functools.partial(near_kernel, dims),
-        out_shape=(field_buffer,) * 3 + (tile,) + (square,) * 4,
+        out_shape=(field_buffer,) * 3
+        + (tile,)
+        + (square,) * 4,
         in_specs=[smem] + [vmem] * len(early),
         out_specs=[vmem] * 8,
         scratch_shapes=[
             pltpu.VMEM((2 * rows_here * len(early), LANES), jnp.float32),
-            pltpu.VMEM((tall, core, nm), jnp.float32),
+            pltpu.VMEM((tall // 2, core, nm), jnp.float32),
         ],
         compiler_params=params,
         cost_estimate=pl.CostEstimate(flops=10**9, bytes_accessed=4 * 10**7, transcendentals=0),
@@ -512,18 +541,22 @@
     )(place, *early)
     n_far = len(far)
     back_block = jax.ShapeDtypeStruct((rows_here * core + tall, nm), jnp.float32)
-    _, _, _, gram1, gram2, ray, coup, field, row0, *back = pl.pallas_call(
+    packed = jax.ShapeDtypeStruct((3 * nm // 2, nm), jnp.float32)
+    _, _, _, packed, ray, coup, field, row0, *back = pl.pallas_call(
         functools.partial(far_kernel, dims),
         out_shape=(field_buffer,) * 3
-        + (square,) * 4
+        + (packed,)
+        + (square,) * 2
         + (tile, jax.ShapeDtypeStruct((core, nm), jnp.float32))
         + (back_block,) * (group - 1),
         in_specs=[smem] + [vmem] * (n_far + 8),
-        out_specs=[vmem] * (8 + group),
+        out_specs=[vmem] * (7 + group),
         input_output_aliases={1 + n_far + i: i for i in range(3)},
         scratch_shapes=[
             pltpu.VMEM((2 * rows_here * n_far, LANES), jnp.float32),
-            pltpu.VMEM((tall, core, nm), jnp.float32),
+            pltpu.VMEM((tall // 2, core, nm), jnp.float32),
+            pltpu.VMEM((nm, nm), jnp.float32),
+            pltpu.VMEM((nm, nm), jnp.float32),
         ],
         compiler_params=params,
         cost_estimate=pl.CostEstimate(flops=10**9, bytes_accessed=2 * 10**7, transcendentals=0),
@@ -531,37 +564,44 @@
     )(place, *far, x, y, weight, start, *sums)
 
     recv = lax.ppermute(field, "cuts", [(i, i + 1) for i in range(cuts - 1)])
-    gram1, gram2 = sum_pair(gram1, gram2, "rows")
-    down = lax.ppermute(row0, "rows", hop(0, True))
+    packed, packed_there = sum_over(packed, "rows")
+    down = lax.ppermute(row0, "rows", hop(0))
     sent = back
     back = []
     for k in range(1, group):
         back.append(xor_swap(sent[k - 1], "rows", k))
 
-    big = min(nm, 32)
+    turned = pl.pallas_call(
+        turn_kernel,
+        out_shape=jax.ShapeDtypeStruct(rotations.shape[1:], jnp.float32),
+        in_specs=[vmem] * 2,
+        out_specs=vmem,
+        compiler_params=grant(2),
+        cost_estimate=pl.CostEstimate(flops=10**8, bytes_accessed=10**6, transcendentals=0),
+        name="turn",
+    )(rotations[0], ordering[0])
+    big = min(nm, 64)
     mix = pl.pallas_call(
         functools.partial(mixing_kernel, 1.0 / pixels),
         out_shape=square,
-        in_specs=[vmem, vmem, pl.BlockSpec(memory_space=pl.ANY), vmem],
+        in_specs=[vmem] * 3,
         out_specs=vmem,
-        compiler_params=params,
+        compiler_params=grant(4),
         cost_estimate=pl.CostEstimate(flops=10**9, bytes_accessed=4 * 10**7, transcendentals=0),
         scratch_shapes=[
-            pltpu.VMEM((nm, 2 * nm), jnp.float32),
-            pltpu.VMEM((big, 2 * nm), jnp.float32),
             pltpu.VMEM((nm, nm), jnp.float32),
-            pltpu.VMEM(rotations.shape[1:], jnp.float32),
-            pltpu.SemaphoreType.DMA,
+            pltpu.VMEM((big, nm), jnp.float32),
+            pltpu.VMEM((nm, nm), jnp.float32),
         ],
         name="mixing",
-    )(gram1, gram2, rotations[0], ordering[0])
+    )(packed, packed_there, turned)
 
     before = lax.ppermute(mix, "cuts", [(i, i + 1) for i in range(cuts - 1)])
     edges = [k for k in range(1, group) if k & (k + 1) == 0]
     beside = [back[k - 1] for k in edges]
     recv, down, beside, mix_now = lax.optimization_barrier((recv, down, beside, mix))
-    turned = q == near - 1
-    turn = [jnp.where(turned, tall - 1, 0), jnp.where(turned, -1, 1)]
+    flip = q == near - 1
+    turn = [jnp.where(flip, tall - 1, 0), jnp.where(flip, -1, 1)]
     turn += [(((q ^ (q + 1)) == k) & (q != group - 1)).astype(jnp.int32) for k in edges]
     turn = jnp.stack(turn)
     ray, coup = pl.pallas_call(
@@ -570,7 +610,7 @@
         in_specs=[smem] + [vmem] * (5 + len(edges)),
         out_specs=[vmem] * 2,
         scratch_shapes=[pltpu.VMEM((tall, nm), jnp.float32)],
-        compiler_params=params,
+        compiler_params=grant(6),
         cost_estimate=pl.CostEstimate(flops=10**9, bytes_accessed=10**7, transcendentals=0),
         name="late",
     )(turn.astype(jnp.int32), field, recv, down, ray, coup, *beside)
@@ -581,7 +621,7 @@
         out_shape=jax.ShapeDtypeStruct((2 * nm, nm), jnp.float32),
         in_specs=[smem] + [vmem] * 4,
         out_specs=vmem,
-        compiler_params=params,
+        compiler_params=grant(4),
         cost_estimate=pl.CostEstimate(flops=10**8, bytes_accessed=10**6, transcendentals=0),
         name="project",
     )(first, ray, coup, before, mix_now)
@@ -605,8 +645,12 @@
         functools.partial(modes_kernel, (rows_here, group, core)),
         out_shape=jax.ShapeDtypeStruct((rows_here, columns, nm), jnp.float32),
         in_specs=[smem] + [vmem] * (group + 1),
-        out_specs=vmem,
-        compiler_params=params,
+        out_specs=hbm,
+        scratch_shapes=[
+            pltpu.VMEM((rows_here, columns, nm), jnp.float32),
+            pltpu.SemaphoreType.DMA((rows_here,)),
+        ],
+        compiler_params=grant(6),
         cost_estimate=pl.CostEstimate(flops=10**9, bytes_accessed=10**7, transcendentals=0),
         name="modes",
     )(where, field, *back, mix)

time: 91.3 us -> 86 us (0.942)
  the two profiles are of different devices: /device:TPU:8 before, /device:TPU:0 now
where the time goes in v1:
time: 86 us; the launch traced here: 85.7 us
  starting transfers between devices  30.8 us (36%)
  waiting for transfers between devices  27.4 us (32%)
  Pallas kernels  21.9 us (25%)
  local copies, waits for them, and re-layouts  4.07 us (5%)
  between operations  1.18 us (1%)
    ppermute x14, waiting for transfers between devices, xor_swap(): return lax.ppermute(value, axis, [(i, i ^ bit) for i in range(peers)])  25.5 us
    ppermute x14, starting transfers between devices, xor_swap(): return lax.ppermute(value, axis, [(i, i ^ bit) for i in range(peers)])  14.6 us
    pallas_call x1, Pallas kernels, body(): pl.pallas_call(functools.partial(mixing_kernel, 1.0 / pixels), out_shape=...  8.87 us
    ppermute x2, starting transfers between devices, body(): lax.ppermute(arrived[k], 'rows', hop(0, True))  7.47 us
    pallas_call x1, Pallas kernels, body(): pl.pallas_call(functools.partial(near_kernel, dims), out_shape=(field_buf...  5.88 us
    pallas_call x1, Pallas kernels, body(): pl.pallas_call(functools.partial(far_kernel, dims), out_shape=(field_buff...  3.49 us
    ppermute x1, starting transfers between devices, body(): recv = lax.ppermute(field, 'cuts', [(i, i + 1) for i in range(cuts - 1)])  3.45 us
    ppermute x2, starting transfers between devices, body(): direct.append(lax.ppermute(windows[j], 'rows', hop(j)))  2.58 us
  transfers between devices with their start and end apart: 21, of which 12 were waited for; matrix products, arithmetic and copies ran while one was open for 1% of the time, Pallas kernels for 21%

profile of v1, /device:TPU:0, one launch (start us, length us, event | category | flops | bytes accessed | tf_op | source)
XLA Modules:
  0.0 85.7 jit_solution(15434074684696131566)
XLA Ops:
  1.6 1.4 %constant_dynamic-slice_fusion = (f32[1,4,144,128]{3,2,1,0:T(8,128)S(1)}, f32[1,4,144,128]{3,2,1,0:T(8,128)S(1)}, f32[1,4,144,128]{3,2,1,0:T(8,128)S(1)}, f32[1,4,144,128]{3,2,1,0:T(8,128)S(1)}) fusion(f32[1,4,512,128]{3,2,1,0:T(8,128)} %param.4, s32[]{:T(128)S(6)} %min.17, s32[]{:T(128)S(6)} %min.16, s32[]{:T(128)S(6)} %min.15, s32[]{:T(128)S(6)} %min.14), kind=kLoop, calls=%fused_computation.18 | loop fusion | bytes 2359312 | tf_op jit(solution)/shard_map/dynamic_slice | solution.py:470
  3.0 3.1 %collective-permute-start = (f32[584,128]{1,0:T(8,128)S(1)}, f32[584,128]{1,0:T(8,128)S(1)}, u32[]{:S(2)}, u32[]{:S(2)}) collective-permute-start(f32[584,128]{1,0:T(8,128)S(1)} %pad_maximum_fusion), channel_id=1, source_target_pairs={{0,2},{1,3},{2,0},{3,1},{4,6},{5,7},{6,4},{7,5},{8,10},{9,11},{10,... | collective-permute-start | bytes 897032 | tf_op jit(solution)/shard_map/ppermute | solution.py:428
  6.5 1.3 %collective-permute-start.5 = (f32[584,128]{1,0:T(8,128)S(1)}, f32[584,128]{1,0:T(8,128)S(1)}, u32[]{:S(2)}, u32[]{:S(2)}) collective-permute-start(f32[584,128]{1,0:T(8,128)S(1)} %pad_maximum_fusion.2.refs_0_), channel_id=1, source_target_pairs={{2,6},{3,7},{4,0},{5,1},{6,10},{7,11},{8,4},{9,5},{10,14},{11,15},... | collective-permute-start | bytes 897032 | tf_op jit(solution)/shard_map/ppermute | solution.py:484
  7.8 1.3 %collective-permute-start.6 = (f32[584,128]{1,0:T(8,128)S(1)}, f32[584,128]{1,0:T(8,128)S(1)}, u32[]{:S(2)}, u32[]{:S(2)}) collective-permute-start(f32[584,128]{1,0:T(8,128)S(1)} %pad_maximum_fusion.3), channel_id=1, source_target_pairs={{2,7},{3,6},{4,1},{5,0},{6,11},{7,10},{8,5},{9,4},{10,15},{11,14},... | collective-permute-start | bytes 897032 | tf_op jit(solution)/shard_map/ppermute | solution.py:484
  9.1 4.9 %collective-permute-done.refs_2_ = f32[584,128]{1,0:T(8,128)S(1)} collective-permute-done((f32[584,128]{1,0:T(8,128)S(1)}, f32[584,128]{1,0:T(8,128)S(1)}, u32[]{:S(2)}, u32[]{:S(2)}) %collective-permute-start) | collective-permute-done | bytes 299040 | tf_op jit(solution)/shard_map/ppermute | solution.py:428
  14.0 4.0 %collective-permute-start.1 = (f32[584,128]{1,0:T(8,128)S(1)}, f32[584,128]{1,0:T(8,128)S(1)}, u32[]{:S(2)}, u32[]{:S(2)}) collective-permute-start(f32[584,128]{1,0:T(8,128)S(1)} %collective-permute-done.refs_2_), channel_id=1, source_target_pairs={{0,4},{1,5},{4,8},{5,9},{6,2},{7,3},{8,12},{9,13},{10,6},{11,7},{1... | collective-permute-start | bytes 897032 | tf_op jit(solution)/shard_map/ppermute | solution.py:485
  18.8 3.5 %collective-permute-start.3 = (f32[584,128]{1,0:T(8,128)S(1)}, f32[584,128]{1,0:T(8,128)S(1)}, u32[]{:S(2)}, u32[]{:S(2)}) collective-permute-start(f32[584,128]{1,0:T(8,128)S(1)} %collective-permute-done.2.refs_3_), channel_id=1, source_target_pairs={{0,4},{1,5},{4,8},{5,9},{6,2},{7,3},{8,12},{9,13},{10,6},{11,7},{1... | collective-permute-start | bytes 897032 | tf_op jit(solution)/shard_map/ppermute | solution.py:485
  23.6 5.9 %near.1 = (f32[32,160,128]{2,1,0:T(8,128)S(1)}, f32[32,160,128]{2,1,0:T(8,128)S(1)}, f32[32,160,128]{2,1,0:T(8,128)S(1)}, f32[16,128,128]{2,1,0:T(8,128)S(1)}, f...) custom-call(s32[18]{0:T(128)S(1)} %stack.156.pos, ...), custom_call_target="tpu_custom_call" | custom-call | flops 1000000000 | bytes 40000000 | tf_op jit(solution)/shard_map/near/pallas_call | solution.py:527
  29.7 3.5 %far.1 = (f32[32,160,128]{2,1,0:T(8,128)S(1)}, f32[32,160,128]{2,1,0:T(8,128)S(1)}, f32[32,160,128]{2,1,0:T(8,128)S(1)}, f32[192,128]{1,0:T(8,128)S(1)}, f32[128...) custom-call(s32[18]{0:T(128)S(1)} %stack.156.pos, ...), custom_call_target="tpu_custom_call", output_to_operand_aliasing={{0}: (3, {}), {1}: (4, {}), {2}: (5, {})} | custom-call | flops 1000000000 | bytes 20000000 | tf_op jit(solution)/shard_map/far/pallas_call | solution.py:545
  33.2 3.4 %collective-permute-start.14 = (f32[16,128,128]{2,1,0:T(8,128)S(1)}, f32[16,128,128]{2,1,0:T(8,128)S(1)}, u32[]{:S(2)}, u32[]{:S(2)}) collective-permute-start(f32[16,128,128]{2,1,0:T(8,128)S(1)} %get-tuple-element.34.refs_0_.out), channel_id=1, source_target_pairs={{0,16},{1,17},{2,18},{3,19},{4,20},{5,21},{6,22},{7,23},{8,24},{9,... | collective-permute-start | bytes 3145736 | tf_op jit(solution)/shard_map/ppermute | solution.py:566
  38.0 4.0 %collective-permute-start.11 = (f32[192,128]{1,0:T(8,128)S(1)}, f32[192,128]{1,0:T(8,128)S(1)}, u32[]{:S(2)}, u32[]{:S(2)}) collective-permute-start(f32[192,128]{1,0:T(8,128)S(1)} %add.95), channel_id=1, source_target_pairs={{0,2},{1,3},{2,0},{3,1},{4,6},{5,7},{6,4},{7,5},{8,10},{9,11},{10,... | collective-permute-start | bytes 294920 | tf_op jit(solution)/shard_map/ppermute | solution.py:428
  42.0 3.1 %collective-permute-done.11 = f32[192,128]{1,0:T(8,128)S(1)} collective-permute-done((f32[192,128]{1,0:T(8,128)S(1)}, f32[192,128]{1,0:T(8,128)S(1)}, u32[]{:S(2)}, u32[]{:S(2)}) %collective-permute-start.11) | collective-permute-done | bytes 98336 | tf_op jit(solution)/shard_map/ppermute | solution.py:428
  45.1 1.6 %collective-permute-start.12 = (f32[192,128]{1,0:T(8,128)S(1)}, f32[192,128]{1,0:T(8,128)S(1)}, u32[]{:S(2)}, u32[]{:S(2)}) collective-permute-start(f32[192,128]{1,0:T(8,128)S(1)} %add.96), channel_id=1, source_target_pairs={{0,4},{1,5},{2,6},{3,7},{4,0},{5,1},{6,2},{7,3},{8,12},{9,13},{10,... | collective-permute-start | bytes 294920 | tf_op jit(solution)/shard_map/ppermute | solution.py:428
  46.8 1.9 %collective-permute-start.9 = (f32[528,128]{1,0:T(8,128)S(1)}, f32[528,128]{1,0:T(8,128)S(1)}, u32[]{:S(2)}, u32[]{:S(2)}) collective-permute-start(f32[528,128]{1,0:T(8,128)S(1)} %get-tuple-element.37), channel_id=1, source_target_pairs={{0,3},{1,2},{2,1},{3,0},{4,7},{5,6},{6,5},{7,4},{8,11},{9,10},{10,... | collective-permute-start | bytes 811016 | tf_op jit(solution)/shard_map/ppermute | solution.py:428
  49.9 2.0 %collective-permute-start.13 = (f32[192,128]{1,0:T(8,128)S(1)}, f32[192,128]{1,0:T(8,128)S(1)}, u32[]{:S(2)}, u32[]{:S(2)}) collective-permute-start(f32[192,128]{1,0:T(8,128)S(1)} %add.97.packed), channel_id=1, source_target_pairs={{0,8},{1,9},{2,10},{3,11},{4,12},{5,13},{6,14},{7,15},{8,0},{9,1},... | collective-permute-start | bytes 294920 | tf_op jit(solution)/shard_map/ppermute | solution.py:428
  51.9 1.5 %collective-permute-start.15 = (f32[128,128]{1,0:T(8,128)}, f32[128,128]{1,0:T(8,128)S(1)}, u32[]{:S(2)}, u32[]{:S(2)}) collective-permute-start(f32[128,128]{1,0:T(8,128)} %copy-done.5), channel_id=1, source_target_pairs={{2,6},{3,7},{4,0},{5,1},{6,10},{7,11},{8,4},{9,5},{10,14},{11,15},... | collective-permute-start | bytes 196616 | tf_op jit(solution)/shard_map/ppermute | solution.py:568
  53.4 4.2 %collective-permute-done.13.there = f32[192,128]{1,0:T(8,128)S(1)} collective-permute-done((f32[192,128]{1,0:T(8,128)S(1)}, f32[192,128]{1,0:T(8,128)S(1)}, u32[]{:S(2)}, u32[]{:S(2)}) %collective-permute-start.13) | collective-permute-done | bytes 98336 | tf_op jit(solution)/shard_map/ppermute | solution.py:428
  57.7 8.9 %mixing.1.refs_4_.mix = f32[128,128]{1,0:T(8,128)S(1)} custom-call(f32[192,128]{1,0:T(8,128)S(1)} %add.97.packed, f32[192,128]{1,0:T(8,128)S(1)} %collective-permute-done.13.there, f32[2,128,128]{2,1,0:T(8,128)S(1)} %turn.1.turned), custom_call_target="tpu_custom_call" | custom-call | flops 1000000000 | bytes 40000000 | tf_op jit(solution)/shard_map/mixing/pallas_call | solution.py:584
  66.5 1.3 %collective-permute-start.16 = (f32[128,128]{1,0:T(8,128)S(1)}, f32[128,128]{1,0:T(8,128)S(1)}, u32[]{:S(2)}, u32[]{:S(2)}) collective-permute-start(f32[128,128]{1,0:T(8,128)S(1)} %mixing.1.refs_4_.mix), channel_id=1, source_target_pairs={{0,16},{1,17},{2,18},{3,19},{4,20},{5,21},{6,22},{7,23},{8,24},{9,... | collective-permute-start | bytes 196616 | tf_op jit(solution)/shard_map/ppermute | solution.py:599
  70.3 1.2 %collective-permute-done.17 = f32[128,128]{1,0:T(8,128)S(1)} collective-permute-done((f32[128,128]{1,0:T(8,128)S(1)}, f32[128,128]{1,0:T(8,128)S(1)}, u32[]{:S(2)}, u32[]{:S(2)}) %collective-permute-start.17) | collective-permute-done | bytes 65568 | tf_op jit(solution)/shard_map/ppermute | solution.py:428
  71.7 3.9 %collective-permute-done.18 = f32[64,128]{1,0:T(8,128)S(1)} collective-permute-done((f32[64,128]{1,0:T(8,128)S(1)}, f32[64,128]{1,0:T(8,128)S(1)}, u32[]{:S(2)}, u32[]{:S(2)}) %collective-permute-start.18) | collective-permute-done | bytes 32800 | tf_op jit(solution)/shard_map/ppermute | solution.py:428
  76.9 2.5 %collective-permute-done.19 = f32[32,128]{1,0:T(8,128)S(1)} collective-permute-done((f32[32,128]{1,0:T(8,128)S(1)}, f32[32,128]{1,0:T(8,128)S(1)}, u32[]{:S(2)}, u32[]{:S(2)}) %collective-permute-start.19) | collective-permute-done | bytes 16416 | tf_op jit(solution)/shard_map/ppermute | solution.py:428
  79.7 3.6 %collective-permute-done.8.refs_2_ = f32[528,128]{1,0:T(8,128)S(1)} collective-permute-done((f32[528,128]{1,0:T(8,128)S(1)}, f32[528,128]{1,0:T(8,128)S(1)}, u32[]{:S(2)}, u32[]{:S(2)}) %collective-permute-start.8) | collective-permute-done | bytes 270368 | tf_op jit(solution)/shard_map/ppermute | solution.py:428
  83.2 1.8 %modes.1 = f32[4,512,128]{2,1,0:T(8,128)} custom-call(s32[12]{0:T(128)S(1)} %stack.135.pos, f32[16,128,128]{2,1,0:T(8,128)S(1)} %get-tuple-element.34.refs_0_.out, f32[528,128]{1,0:T(8,128)S(1)} %collective-permute-done.7.refs_1_.refs_0_, f32[528,128]{1,0:T(8,128)S(1)} %collective-permute-done.8.refs_2_, ...), custom_call_target="tpu_custom_call" | custom-call | flops 1000000000 | bytes 10000000 | tf_op jit(solution)/shard_map/modes/pallas_call | solution.py:644
  (68 shorter events, 10.8 us)
Async XLA Ops:
  3.0 11.0 %collective-permute-start = (f32[584,128]{1,0:T(8,128)S(1)}, f32[584,128]{1,0:T(8,128)S(1)}, u32[]{:S(2)}, u32[]{:S(2)}) collective-permute-start(f32[584,128]{1,0:T(8,128)S(1)} %pad_maximum_fusion), channel_id=1, source_target_pairs={{0,2},{1,3},{2,0},{3,1},{4,6},{5,7},{6,4},{7,5},{8,10},{9,11},{10,... | collective-permute-start | bytes 897032 | tf_op jit(solution)/shard_map/ppermute | solution.py:428
  6.1 12.7 %collective-permute-start.2 = (f32[584,128]{1,0:T(8,128)S(1)}, f32[584,128]{1,0:T(8,128)S(1)}, u32[]{:S(2)}, u32[]{:S(2)}) collective-permute-start(f32[584,128]{1,0:T(8,128)S(1)} %pad_maximum_fusion.1), channel_id=1, source_target_pairs={{0,3},{1,2},{2,1},{3,0},{4,7},{5,6},{6,5},{7,4},{8,11},{9,10},{10,... | collective-permute-start | bytes 897032 | tf_op jit(solution)/shard_map/ppermute | solution.py:428
  6.3 16.3 %collective-permute-start.4 = (f32[584,128]{1,0:T(8,128)S(1)}, f32[584,128]{1,0:T(8,128)S(1)}, u32[]{:S(2)}, u32[]{:S(2)}) collective-permute-start(f32[584,128]{1,0:T(8,128)S(1)} %pad_maximum_fusion.3), channel_id=1, source_target_pairs={{0,1},{1,0},{2,3},{3,2},{4,5},{5,4},{6,7},{7,6},{8,9},{9,8},{10,11... | collective-permute-start | bytes 897032 | tf_op jit(solution)/shard_map/ppermute | solution.py:428
  6.5 16.1 %collective-permute-start.5 = (f32[584,128]{1,0:T(8,128)S(1)}, f32[584,128]{1,0:T(8,128)S(1)}, u32[]{:S(2)}, u32[]{:S(2)}) collective-permute-start(f32[584,128]{1,0:T(8,128)S(1)} %pad_maximum_fusion.2.refs_0_), channel_id=1, source_target_pairs={{2,6},{3,7},{4,0},{5,1},{6,10},{7,11},{8,4},{9,5},{10,14},{11,15},... | collective-permute-start | bytes 897032 | tf_op jit(solution)/shard_map/ppermute | solution.py:484
  7.8 15.8 %collective-permute-start.6 = (f32[584,128]{1,0:T(8,128)S(1)}, f32[584,128]{1,0:T(8,128)S(1)}, u32[]{:S(2)}, u32[]{:S(2)}) collective-permute-start(f32[584,128]{1,0:T(8,128)S(1)} %pad_maximum_fusion.3), channel_id=1, source_target_pairs={{2,7},{3,6},{4,1},{5,0},{6,11},{7,10},{8,5},{9,4},{10,15},{11,14},... | collective-permute-start | bytes 897032 | tf_op jit(solution)/shard_map/ppermute | solution.py:484
  14.0 15.4 %collective-permute-start.1 = (f32[584,128]{1,0:T(8,128)S(1)}, f32[584,128]{1,0:T(8,128)S(1)}, u32[]{:S(2)}, u32[]{:S(2)}) collective-permute-start(f32[584,128]{1,0:T(8,128)S(1)} %collective-permute-done.refs_2_), channel_id=1, source_target_pairs={{0,4},{1,5},{4,8},{5,9},{6,2},{7,3},{8,12},{9,13},{10,6},{11,7},{1... | collective-permute-start | bytes 897032 | tf_op jit(solution)/shard_map/ppermute | solution.py:485
  18.8 10.8 %collective-permute-start.3 = (f32[584,128]{1,0:T(8,128)S(1)}, f32[584,128]{1,0:T(8,128)S(1)}, u32[]{:S(2)}, u32[]{:S(2)}) collective-permute-start(f32[584,128]{1,0:T(8,128)S(1)} %collective-permute-done.2.refs_3_), channel_id=1, source_target_pairs={{0,4},{1,5},{4,8},{5,9},{6,2},{7,3},{8,12},{9,13},{10,6},{11,7},{1... | collective-permute-start | bytes 897032 | tf_op jit(solution)/shard_map/ppermute | solution.py:485
  29.7 19.0 %copy-start.6 = (s32[1,2,128]{2,1,0:T(2,128)S(1)}, s32[1,2,128]{2,1,0:T(2,128)}, u32[]{:S(2)}) copy-start(s32[1,2,128]{2,1,0:T(2,128)} %param.7) | copy-start | bytes 3076
  33.2 34.7 %collective-permute-start.14 = (f32[16,128,128]{2,1,0:T(8,128)S(1)}, f32[16,128,128]{2,1,0:T(8,128)S(1)}, u32[]{:S(2)}, u32[]{:S(2)}) collective-permute-start(f32[16,128,128]{2,1,0:T(8,128)S(1)} %get-tuple-element.34.refs_0_.out), channel_id=1, source_target_pairs={{0,16},{1,17},{2,18},{3,19},{4,20},{5,21},{6,22},{7,23},{8,24},{9,... | collective-permute-start | bytes 3145736 | tf_op jit(solution)/shard_map/ppermute | solution.py:566
  36.6 1.4 %collective-permute-start.10 = (f32[192,128]{1,0:T(8,128)S(1)}, f32[192,128]{1,0:T(8,128)S(1)}, u32[]{:S(2)}, u32[]{:S(2)}) collective-permute-start(f32[192,128]{1,0:T(8,128)S(1)} %get-tuple-element.38), channel_id=1, source_target_pairs={{0,1},{1,0},{2,3},{3,2},{4,5},{5,4},{6,7},{7,6},{8,9},{9,8},{10,11... | collective-permute-start | bytes 294920 | tf_op jit(solution)/shard_map/ppermute | solution.py:428
  38.0 7.1 %collective-permute-start.11 = (f32[192,128]{1,0:T(8,128)S(1)}, f32[192,128]{1,0:T(8,128)S(1)}, u32[]{:S(2)}, u32[]{:S(2)}) collective-permute-start(f32[192,128]{1,0:T(8,128)S(1)} %add.95), channel_id=1, source_target_pairs={{0,2},{1,3},{2,0},{3,1},{4,6},{5,7},{6,4},{7,5},{8,10},{9,11},{10,... | collective-permute-start | bytes 294920 | tf_op jit(solution)/shard_map/ppermute | solution.py:428
  45.1 4.7 %collective-permute-start.12 = (f32[192,128]{1,0:T(8,128)S(1)}, f32[192,128]{1,0:T(8,128)S(1)}, u32[]{:S(2)}, u32[]{:S(2)}) collective-permute-start(f32[192,128]{1,0:T(8,128)S(1)} %add.96), channel_id=1, source_target_pairs={{0,4},{1,5},{2,6},{3,7},{4,0},{5,1},{6,2},{7,3},{8,12},{9,13},{10,... | collective-permute-start | bytes 294920 | tf_op jit(solution)/shard_map/ppermute | solution.py:428
  46.7 21.1 %collective-permute-start.7 = (f32[528,128]{1,0:T(8,128)}, f32[528,128]{1,0:T(8,128)S(1)}, u32[]{:S(2)}, u32[]{:S(2)}) collective-permute-start(f32[528,128]{1,0:T(8,128)} %get-tuple-element.35), channel_id=1, source_target_pairs={{0,1},{1,0},{2,3},{3,2},{4,5},{5,4},{6,7},{7,6},{8,9},{9,8},{10,11... | collective-permute-start | bytes 811016 | tf_op jit(solution)/shard_map/ppermute | solution.py:428
  46.8 21.1 %collective-permute-start.9 = (f32[528,128]{1,0:T(8,128)S(1)}, f32[528,128]{1,0:T(8,128)S(1)}, u32[]{:S(2)}, u32[]{:S(2)}) collective-permute-start(f32[528,128]{1,0:T(8,128)S(1)} %get-tuple-element.37), channel_id=1, source_target_pairs={{0,3},{1,2},{2,1},{3,0},{4,7},{5,6},{6,5},{7,4},{8,11},{9,10},{10,... | collective-permute-start | bytes 811016 | tf_op jit(solution)/shard_map/ppermute | solution.py:428
  49.6 18.3 %copy-start.2 = (f32[128,128]{1,0:T(8,128)S(1)}, f32[128,128]{1,0:T(8,128)}, u32[]{:S(2)}) copy-start(f32[128,128]{1,0:T(8,128)} %copy-done.1) | copy-start | bytes 196612
  49.6 18.3 %copy-start.4 = (f32[128,128]{1,0:T(8,128)S(1)}, f32[128,128]{1,0:T(8,128)}, u32[]{:S(2)}) copy-start(f32[128,128]{1,0:T(8,128)} %copy-done.3) | copy-start | bytes 196612
  49.9 7.8 %collective-permute-start.13 = (f32[192,128]{1,0:T(8,128)S(1)}, f32[192,128]{1,0:T(8,128)S(1)}, u32[]{:S(2)}, u32[]{:S(2)}) collective-permute-start(f32[192,128]{1,0:T(8,128)S(1)} %add.97.packed), channel_id=1, source_target_pairs={{0,8},{1,9},{2,10},{3,11},{4,12},{5,13},{6,14},{7,15},{8,0},{9,1},... | collective-permute-start | bytes 294920 | tf_op jit(solution)/shard_map/ppermute | solution.py:428
  51.9 15.9 %collective-permute-start.15 = (f32[128,128]{1,0:T(8,128)}, f32[128,128]{1,0:T(8,128)S(1)}, u32[]{:S(2)}, u32[]{:S(2)}) collective-permute-start(f32[128,128]{1,0:T(8,128)} %copy-done.5), channel_id=1, source_target_pairs={{2,6},{3,7},{4,0},{5,1},{6,10},{7,11},{8,4},{9,5},{10,14},{11,15},... | collective-permute-start | bytes 196616 | tf_op jit(solution)/shard_map/ppermute | solution.py:568
  66.5 3.2 %collective-permute-start.16 = (f32[128,128]{1,0:T(8,128)S(1)}, f32[128,128]{1,0:T(8,128)S(1)}, u32[]{:S(2)}, u32[]{:S(2)}) collective-permute-start(f32[128,128]{1,0:T(8,128)S(1)} %mixing.1.refs_4_.mix), channel_id=1, source_target_pairs={{0,16},{1,17},{2,18},{3,19},{4,20},{5,21},{6,22},{7,23},{8,24},{9,... | collective-permute-start | bytes 196616 | tf_op jit(solution)/shard_map/ppermute | solution.py:599
  70.2 1.3 %collective-permute-start.17 = (f32[128,128]{1,0:T(8,128)S(1)}, f32[128,128]{1,0:T(8,128)S(1)}, u32[]{:S(2)}, u32[]{:S(2)}) collective-permute-start(f32[128,128]{1,0:T(8,128)S(1)} %slice_select_fusion), channel_id=1, source_target_pairs={{0,1},{1,0},{2,3},{3,2},{4,5},{5,4},{6,7},{7,6},{8,9},{9,8},{10,11... | collective-permute-start | bytes 196616 | tf_op jit(solution)/shard_map/ppermute | solution.py:428
  71.6 4.0 %collective-permute-start.18 = (f32[64,128]{1,0:T(8,128)S(1)}, f32[64,128]{1,0:T(8,128)S(1)}, u32[]{:S(2)}, u32[]{:S(2)}) collective-permute-start(f32[64,128]{1,0:T(8,128)S(1)} %slice_select_fusion.1), channel_id=1, source_target_pairs={{0,2},{1,3},{2,0},{3,1},{4,6},{5,7},{6,4},{7,5},{8,10},{9,11},{10,... | collective-permute-start | bytes 98312 | tf_op jit(solution)/shard_map/ppermute | solution.py:428
  75.6 3.8 %collective-permute-start.19 = (f32[32,128]{1,0:T(8,128)S(1)}, f32[32,128]{1,0:T(8,128)S(1)}, u32[]{:S(2)}, u32[]{:S(2)}) collective-permute-start(f32[32,128]{1,0:T(8,128)S(1)} %slice_select_fusion.2), channel_id=1, source_target_pairs={{0,4},{1,5},{2,6},{3,7},{4,0},{5,1},{6,2},{7,3},{8,12},{9,13},{10,... | collective-permute-start | bytes 49160 | tf_op jit(solution)/shard_map/ppermute | solution.py:428
  75.8 7.5 %collective-permute-start.8 = (f32[528,128]{1,0:T(8,128)S(1)}, f32[528,128]{1,0:T(8,128)S(1)}, u32[]{:S(2)}, u32[]{:S(2)}) collective-permute-start(f32[528,128]{1,0:T(8,128)S(1)} %get-tuple-element.36), channel_id=1, source_target_pairs={{0,2},{1,3},{2,0},{3,1},{4,6},{5,7},{6,4},{7,5},{8,10},{9,11},{10,... | collective-permute-start | bytes 811016 | tf_op jit(solution)/shard_map/ppermute | solution.py:428
  79.4 5.7 %collective-permute-start.20 = (f32[16,128]{1,0:T(8,128)S(1)}, f32[16,128]{1,0:T(8,128)S(1)}, u32[]{:S(2)}, u32[]{:S(2)}) collective-permute-start(f32[16,128]{1,0:T(8,128)S(1)} %slice_select_fusion.3), channel_id=1, source_target_pairs={{0,8},{1,9},{2,10},{3,11},{4,12},{5,13},{6,14},{7,15},{8,0},{9,1},... | collective-permute-start | bytes 24584 | tf_op jit(solution)/shard_map/ppermute | solution.py:428
  (4 other events, 41.6 us)

commit v2 on v1

--- a/solution.py
+++ b/solution.py
@@ -380,13 +380,6 @@
     mix[...] = mm(m1, m2)
 
 
-def reversed_bits(value, count):
-    out = 0
-    while count > 1:
-        out, value, count = 2 * out + value % 2, value // 2, count // 2
-    return out
-
-
 def project_kernel(peers, scale, first, ray, coup, before, mix, shares):
     nm = mix.shape[0]
     share = nm // peers
@@ -394,7 +387,7 @@
 
     def place(value, at):
         for r in range(peers):
-            to = (2 * reversed_bits(r, peers) + at) * share
+            to = (2 * r + at) * share
             shares[to : to + share, :] = value[r * share : (r + 1) * share, :]
 
     place(mm_t(mix[...], mm(ray[...] + ray[...].T, m)), 1)
@@ -407,20 +400,6 @@
     @pl.when(first[0] != 1)
     def _():
         place(mm_t(before[...], half), 0)
-
-
-def scatter_sum(value, axis):
-    peers = lax.axis_size(axis)
-    me = lax.axis_index(axis)
-    bit = 1
-    while bit < peers:
-        half = value.shape[0] // 2
-        odd = (me & bit) != 0
-        low, high = value[:half], value[half:]
-        other = xor_swap(jnp.where(odd, low, high), axis, bit)
-        value = jnp.where(odd, high, low) + other
-        bit *= 2
-    return value
 
 
 def xor_swap(value, axis, bit):
@@ -625,7 +604,8 @@
         cost_estimate=pl.CostEstimate(flops=10**8, bytes_accessed=10**6, transcendentals=0),
         name="project",
     )(first, ray, coup, before, mix_now)
-    shares = scatter_sum(shares, "rows")
+    shares = shares.reshape(peers, 2 * share, nm)
+    shares = lax.all_to_all(shares, "rows", 0, 0).sum(0)
     coupling, rayleigh = shares[:share], shares[share:]
 
     where = []

time: 86 us -> 86.4 us (level)
  waiting for transfers between devices: 27.4 us -> 21.9 us
  starting transfers between devices: 30.8 us -> 34.7 us
  Pallas kernels: 21.9 us -> 23 us
    ppermute x14 -> x10, waiting for transfers between devices: 25.5 us -> 14.5 us  [xor_swap(): return lax.ppermute(value, axis, [(i, i ^ bit) for i in range(peers)])]
    all_to_all x0 -> x1, waiting for transfers between devices: none -> 5.54 us  [body(): shares = lax.all_to_all(shares, 'rows', 0, 0).sum(0)]
    all_to_all x0 -> x1, starting transfers between devices: none -> 4.27 us  [body(): shares = lax.all_to_all(shares, 'rows', 0, 0).sum(0)]
    add x3, other arithmetic: 0.04 us -> 0.94 us  [sum_over(): value = value + there]
    ppermute x14 -> x10, starting transfers between devices: 14.6 us -> 14.2 us  [xor_swap(): return lax.ppermute(value, axis, [(i, i ^ bit) for i in range(peers)])]
  transfers between devices with their start and end apart: 21 -> 18, of which waited for: 12 -> 10; matrix products, arithmetic and copies ran while one was open for 1% -> 2% of each run, Pallas kernels for 21% -> 23%
where the time goes in v2:
time: 86.4 us; the launch traced here: 85.9 us
  starting transfers between devices  34.7 us (40%)
  Pallas kernels  23 us (27%)
  waiting for transfers between devices  21.9 us (25%)
  local copies, waits for them, and re-layouts  4.07 us (5%)
  other arithmetic  1.12 us (1%)
  between operations  1.1 us (1%)
    ppermute x10, waiting for transfers between devices, xor_swap(): return lax.ppermute(value, axis, [(i, i ^ bit) for i in range(peers)])  14.5 us
    ppermute x10, starting transfers between devices, xor_swap(): return lax.ppermute(value, axis, [(i, i ^ bit) for i in range(peers)])  14.2 us
    pallas_call x1, Pallas kernels, body(): pl.pallas_call(functools.partial(mixing_kernel, 1.0 / pixels), out_shape=...  8.87 us
    ppermute x2, starting transfers between devices, body(): lax.ppermute(arrived[k], 'rows', hop(0, True))  7.47 us
    pallas_call x1, Pallas kernels, body(): pl.pallas_call(functools.partial(near_kernel, dims), out_shape=(field_buf...  5.89 us
    all_to_all x1, waiting for transfers between devices, body(): shares = lax.all_to_all(shares, 'rows', 0, 0).sum(0)  5.54 us
    all_to_all x1, starting transfers between devices, body(): shares = lax.all_to_all(shares, 'rows', 0, 0).sum(0)  4.27 us
    pallas_call x1, Pallas kernels, body(): pl.pallas_call(functools.partial(far_kernel, dims), out_shape=(field_buff...  3.49 us
  transfers between devices with their start and end apart: 18, of which 10 were waited for; matrix products, arithmetic and copies ran while one was open for 2% of the time, Pallas kernels for 23%

profile of v2, /device:TPU:0, one launch (start us, length us, event | category | flops | bytes accessed | tf_op | source)
XLA Modules:
  0.0 85.9 jit_solution(13688575933745743821)
XLA Ops:
  1.6 1.4 %constant_dynamic-slice_fusion = (f32[1,4,144,128]{3,2,1,0:T(8,128)S(1)}, f32[1,4,144,128]{3,2,1,0:T(8,128)S(1)}, f32[1,4,144,128]{3,2,1,0:T(8,128)S(1)}, f32[1,4,144,128]{3,2,1,0:T(8,128)S(1)}) fusion(f32[1,4,512,128]{3,2,1,0:T(8,128)} %param.4, s32[]{:T(128)S(6)} %min.17, s32[]{:T(128)S(6)} %min.16, s32[]{:T(128)S(6)} %min.15, s32[]{:T(128)S(6)} %min.14), kind=kLoop, calls=%fused_computation.10 | loop fusion | bytes 2359312 | tf_op jit(solution)/shard_map/dynamic_slice | solution.py:449
  3.0 3.1 %collective-permute-start = (f32[584,128]{1,0:T(8,128)S(1)}, f32[584,128]{1,0:T(8,128)S(1)}, u32[]{:S(2)}, u32[]{:S(2)}) collective-permute-start(f32[584,128]{1,0:T(8,128)S(1)} %pad_maximum_fusion), channel_id=1, source_target_pairs={{0,2},{1,3},{2,0},{3,1},{4,6},{5,7},{6,4},{7,5},{8,10},{9,11},{10,... | collective-permute-start | bytes 897032 | tf_op jit(solution)/shard_map/ppermute | solution.py:407
  6.5 1.3 %collective-permute-start.5 = (f32[584,128]{1,0:T(8,128)S(1)}, f32[584,128]{1,0:T(8,128)S(1)}, u32[]{:S(2)}, u32[]{:S(2)}) collective-permute-start(f32[584,128]{1,0:T(8,128)S(1)} %pad_maximum_fusion.2.refs_0_), channel_id=1, source_target_pairs={{2,6},{3,7},{4,0},{5,1},{6,10},{7,11},{8,4},{9,5},{10,14},{11,15},... | collective-permute-start | bytes 897032 | tf_op jit(solution)/shard_map/ppermute | solution.py:463
  7.8 1.3 %collective-permute-start.6 = (f32[584,128]{1,0:T(8,128)S(1)}, f32[584,128]{1,0:T(8,128)S(1)}, u32[]{:S(2)}, u32[]{:S(2)}) collective-permute-start(f32[584,128]{1,0:T(8,128)S(1)} %pad_maximum_fusion.3), channel_id=1, source_target_pairs={{2,7},{3,6},{4,1},{5,0},{6,11},{7,10},{8,5},{9,4},{10,15},{11,14},... | collective-permute-start | bytes 897032 | tf_op jit(solution)/shard_map/ppermute | solution.py:463
  9.1 4.9 %collective-permute-done.refs_2_ = f32[584,128]{1,0:T(8,128)S(1)} collective-permute-done((f32[584,128]{1,0:T(8,128)S(1)}, f32[584,128]{1,0:T(8,128)S(1)}, u32[]{:S(2)}, u32[]{:S(2)}) %collective-permute-start) | collective-permute-done | bytes 299040 | tf_op jit(solution)/shard_map/ppermute | solution.py:407
  14.0 4.0 %collective-permute-start.1 = (f32[584,128]{1,0:T(8,128)S(1)}, f32[584,128]{1,0:T(8,128)S(1)}, u32[]{:S(2)}, u32[]{:S(2)}) collective-permute-start(f32[584,128]{1,0:T(8,128)S(1)} %collective-permute-done.refs_2_), channel_id=1, source_target_pairs={{0,4},{1,5},{4,8},{5,9},{6,2},{7,3},{8,12},{9,13},{10,6},{11,7},{1... | collective-permute-start | bytes 897032 | tf_op jit(solution)/shard_map/ppermute | solution.py:464
  18.8 3.5 %collective-permute-start.3 = (f32[584,128]{1,0:T(8,128)S(1)}, f32[584,128]{1,0:T(8,128)S(1)}, u32[]{:S(2)}, u32[]{:S(2)}) collective-permute-start(f32[584,128]{1,0:T(8,128)S(1)} %collective-permute-done.2.refs_3_), channel_id=1, source_target_pairs={{0,4},{1,5},{4,8},{5,9},{6,2},{7,3},{8,12},{9,13},{10,6},{11,7},{1... | collective-permute-start | bytes 897032 | tf_op jit(solution)/shard_map/ppermute | solution.py:464
  23.6 5.9 %near.1 = (f32[32,160,128]{2,1,0:T(8,128)S(1)}, f32[32,160,128]{2,1,0:T(8,128)S(1)}, f32[32,160,128]{2,1,0:T(8,128)S(1)}, f32[16,128,128]{2,1,0:T(8,128)S(1)}, f...) custom-call(s32[18]{0:T(128)S(1)} %stack.156.pos, ...), custom_call_target="tpu_custom_call" | custom-call | flops 1000000000 | bytes 40000000 | tf_op jit(solution)/shard_map/near/pallas_call | solution.py:506
  29.7 3.5 %far.1 = (f32[32,160,128]{2,1,0:T(8,128)S(1)}, f32[32,160,128]{2,1,0:T(8,128)S(1)}, f32[32,160,128]{2,1,0:T(8,128)S(1)}, f32[192,128]{1,0:T(8,128)S(1)}, f32[128...) custom-call(s32[18]{0:T(128)S(1)} %stack.156.pos, ...), custom_call_target="tpu_custom_call", output_to_operand_aliasing={{0}: (3, {}), {1}: (4, {}), {2}: (5, {})} | custom-call | flops 1000000000 | bytes 20000000 | tf_op jit(solution)/shard_map/far/pallas_call | solution.py:524
  33.2 3.5 %collective-permute-start.14 = (f32[16,128,128]{2,1,0:T(8,128)S(1)}, f32[16,128,128]{2,1,0:T(8,128)S(1)}, u32[]{:S(2)}, u32[]{:S(2)}) collective-permute-start(f32[16,128,128]{2,1,0:T(8,128)S(1)} %get-tuple-element.34.refs_0_.out), channel_id=1, source_target_pairs={{0,16},{1,17},{2,18},{3,19},{4,20},{5,21},{6,22},{7,23},{8,24},{9,... | collective-permute-start | bytes 3145736 | tf_op jit(solution)/shard_map/ppermute | solution.py:545
  36.8 1.2 %collective-permute-done.10 = f32[192,128]{1,0:T(8,128)S(1)} collective-permute-done((f32[192,128]{1,0:T(8,128)S(1)}, f32[192,128]{1,0:T(8,128)S(1)}, u32[]{:S(2)}, u32[]{:S(2)}) %collective-permute-start.10) | collective-permute-done | bytes 98336 | tf_op jit(solution)/shard_map/ppermute | solution.py:407
  38.0 4.0 %collective-permute-start.11 = (f32[192,128]{1,0:T(8,128)S(1)}, f32[192,128]{1,0:T(8,128)S(1)}, u32[]{:S(2)}, u32[]{:S(2)}) collective-permute-start(f32[192,128]{1,0:T(8,128)S(1)} %add.83), channel_id=1, source_target_pairs={{0,2},{1,3},{2,0},{3,1},{4,6},{5,7},{6,4},{7,5},{8,10},{9,11},{10,... | collective-permute-start | bytes 294920 | tf_op jit(solution)/shard_map/ppermute | solution.py:407
  42.0 3.1 %collective-permute-done.11 = f32[192,128]{1,0:T(8,128)S(1)} collective-permute-done((f32[192,128]{1,0:T(8,128)S(1)}, f32[192,128]{1,0:T(8,128)S(1)}, u32[]{:S(2)}, u32[]{:S(2)}) %collective-permute-start.11) | collective-permute-done | bytes 98336 | tf_op jit(solution)/shard_map/ppermute | solution.py:407
  45.1 1.6 %collective-permute-start.12 = (f32[192,128]{1,0:T(8,128)S(1)}, f32[192,128]{1,0:T(8,128)}, u32[]{:S(2)}, u32[]{:S(2)}) collective-permute-start(f32[192,128]{1,0:T(8,128)S(1)} %add.84), channel_id=1, source_target_pairs={{0,4},{1,5},{2,6},{3,7},{4,0},{5,1},{6,2},{7,3},{8,12},{9,13},{10,... | collective-permute-start | bytes 294920 | tf_op jit(solution)/shard_map/ppermute | solution.py:407
  46.8 1.9 %collective-permute-start.9 = (f32[528,128]{1,0:T(8,128)S(1)}, f32[528,128]{1,0:T(8,128)S(1)}, u32[]{:S(2)}, u32[]{:S(2)}) collective-permute-start(f32[528,128]{1,0:T(8,128)S(1)} %get-tuple-element.37), channel_id=1, source_target_pairs={{0,3},{1,2},{2,1},{3,0},{4,7},{5,6},{6,5},{7,4},{8,11},{9,10},{10,... | collective-permute-start | bytes 811016 | tf_op jit(solution)/shard_map/ppermute | solution.py:407
  50.8 2.1 %collective-permute-start.13 = (f32[192,128]{1,0:T(8,128)S(1)}, f32[192,128]{1,0:T(8,128)S(1)}, u32[]{:S(2)}, u32[]{:S(2)}) collective-permute-start(f32[192,128]{1,0:T(8,128)S(1)} %add.85.packed), channel_id=1, source_target_pairs={{0,8},{1,9},{2,10},{3,11},{4,12},{5,13},{6,14},{7,15},{8,0},{9,1},... | collective-permute-start | bytes 294920 | tf_op jit(solution)/shard_map/ppermute | solution.py:407
  54.1 4.4 %collective-permute-done.13.there = f32[192,128]{1,0:T(8,128)S(1)} collective-permute-done((f32[192,128]{1,0:T(8,128)S(1)}, f32[192,128]{1,0:T(8,128)S(1)}, u32[]{:S(2)}, u32[]{:S(2)}) %collective-permute-start.13) | collective-permute-done | bytes 98336 | tf_op jit(solution)/shard_map/ppermute | solution.py:407
  58.4 1.5 %collective-permute-start.15 = (f32[128,128]{1,0:T(8,128)}, f32[128,128]{1,0:T(8,128)S(1)}, u32[]{:S(2)}, u32[]{:S(2)}) collective-permute-start(f32[128,128]{1,0:T(8,128)} %copy-done.5), channel_id=1, source_target_pairs={{2,6},{3,7},{4,0},{5,1},{6,10},{7,11},{8,4},{9,5},{10,14},{11,15},... | collective-permute-start | bytes 196616 | tf_op jit(solution)/shard_map/ppermute | solution.py:547
  59.9 8.9 %mixing.1.refs_4_.mix = f32[128,128]{1,0:T(8,128)S(1)} custom-call(f32[192,128]{1,0:T(8,128)S(1)} %add.85.packed, f32[192,128]{1,0:T(8,128)S(1)} %collective-permute-done.13.there, f32[2,128,128]{2,1,0:T(8,128)S(1)} %turn.1.turned), custom_call_target="tpu_custom_call" | custom-call | flops 1000000000 | bytes 40000000 | tf_op jit(solution)/shard_map/mixing/pallas_call | solution.py:563
  68.8 1.3 %collective-permute-start.16 = (f32[128,128]{1,0:T(8,128)S(1)}, f32[128,128]{1,0:T(8,128)S(1)}, u32[]{:S(2)}, u32[]{:S(2)}) collective-permute-start(f32[128,128]{1,0:T(8,128)S(1)} %mixing.1.refs_4_.mix), channel_id=1, source_target_pairs={{0,16},{1,17},{2,18},{3,19},{4,20},{5,21},{6,22},{7,23},{8,24},{9,... | collective-permute-start | bytes 196616 | tf_op jit(solution)/shard_map/ppermute | solution.py:578
  70.2 1.2 %late.1 = (f32[128,128]{1,0:T(8,128)S(1)}, f32[128,128]{1,0:T(8,128)S(1)}) custom-call(s32[4]{0:T(128)S(1)} %pad_add_fusion.turn, f32[16,128,128]{2,1,0:T(8,128)S(1)} %get-tuple-element.34.refs_0_.out, f32[16,128,128]{2,1,0:T(8,128)S(1)} %collective-permute-done.14.recv, f32[128,128]{1,0:T(8,128)S(1)} %collective-permute-done.15.down, ...), custom_call_target="tpu_custom_call" | custom-call | flops 1000000000 | bytes 10000000 | tf_op jit(solution)/shard_map/late/pallas_call | solution.py:586
  73.1 4.3 %all-to-all-start = ((f32[16,16,128]{2,1,0:T(8,128)}), f32[16,16,128]{2,1,0:T(8,128)S(1)}, u32[]{:S(2)}, u32[]{:S(2)}) async-start(f32[16,16,128]{2,1,0:T(8,128)} %bitcast.44), calls=%async_computation | async-start | bytes 262144 | tf_op jit(solution)/shard_map/all_to_all | solution.py:608
  77.5 2.2 %modes.1 = f32[4,512,128]{2,1,0:T(8,128)} custom-call(s32[12]{0:T(128)S(1)} %stack.135.pos, f32[16,128,128]{2,1,0:T(8,128)S(1)} %get-tuple-element.34.refs_0_.out, f32[528,128]{1,0:T(8,128)S(1)} %collective-permute-done.7.refs_1_.refs_0_, f32[528,128]{1,0:T(8,128)} %collective-permute-done.8.refs_2_, f32[528,128]{1,0:T(8,128)S(1)} %collective-permute-done.9.refs_3_.refs_1_, ...), custom_call_target="tpu_custom_call" | custom-call | flops 1000000000 | bytes 10000000 | tf_op jit(solution)/shard_map/modes/pallas_call | solution.py:624
  79.8 5.5 %all-to-all-done = f32[16,16,128]{2,1,0:T(8,128)S(1)} async-done(((f32[16,16,128]{2,1,0:T(8,128)}), f32[16,16,128]{2,1,0:T(8,128)S(1)}, u32[]{:S(2)}, u32[]{:S(2)}) %all-to-all-start) | async-done | bytes 131104 | tf_op jit(solution)/shard_map/all_to_all | solution.py:608
  (55 shorter events, 9.5 us)
Async XLA Ops:
  3.0 11.0 %collective-permute-start = (f32[584,128]{1,0:T(8,128)S(1)}, f32[584,128]{1,0:T(8,128)S(1)}, u32[]{:S(2)}, u32[]{:S(2)}) collective-permute-start(f32[584,128]{1,0:T(8,128)S(1)} %pad_maximum_fusion), channel_id=1, source_target_pairs={{0,2},{1,3},{2,0},{3,1},{4,6},{5,7},{6,4},{7,5},{8,10},{9,11},{10,... | collective-permute-start | bytes 897032 | tf_op jit(solution)/shard_map/ppermute | solution.py:407
  6.1 12.7 %collective-permute-start.2 = (f32[584,128]{1,0:T(8,128)S(1)}, f32[584,128]{1,0:T(8,128)S(1)}, u32[]{:S(2)}, u32[]{:S(2)}) collective-permute-start(f32[584,128]{1,0:T(8,128)S(1)} %pad_maximum_fusion.1), channel_id=1, source_target_pairs={{0,3},{1,2},{2,1},{3,0},{4,7},{5,6},{6,5},{7,4},{8,11},{9,10},{10,... | collective-permute-start | bytes 897032 | tf_op jit(solution)/shard_map/ppermute | solution.py:407
  6.3 16.3 %collective-permute-start.4 = (f32[584,128]{1,0:T(8,128)S(1)}, f32[584,128]{1,0:T(8,128)S(1)}, u32[]{:S(2)}, u32[]{:S(2)}) collective-permute-start(f32[584,128]{1,0:T(8,128)S(1)} %pad_maximum_fusion.3), channel_id=1, source_target_pairs={{0,1},{1,0},{2,3},{3,2},{4,5},{5,4},{6,7},{7,6},{8,9},{9,8},{10,11... | collective-permute-start | bytes 897032 | tf_op jit(solution)/shard_map/ppermute | solution.py:407
  6.5 16.1 %collective-permute-start.5 = (f32[584,128]{1,0:T(8,128)S(1)}, f32[584,128]{1,0:T(8,128)S(1)}, u32[]{:S(2)}, u32[]{:S(2)}) collective-permute-start(f32[584,128]{1,0:T(8,128)S(1)} %pad_maximum_fusion.2.refs_0_), channel_id=1, source_target_pairs={{2,6},{3,7},{4,0},{5,1},{6,10},{7,11},{8,4},{9,5},{10,14},{11,15},... | collective-permute-start | bytes 897032 | tf_op jit(solution)/shard_map/ppermute | solution.py:463
  7.8 15.8 %collective-permute-start.6 = (f32[584,128]{1,0:T(8,128)S(1)}, f32[584,128]{1,0:T(8,128)S(1)}, u32[]{:S(2)}, u32[]{:S(2)}) collective-permute-start(f32[584,128]{1,0:T(8,128)S(1)} %pad_maximum_fusion.3), channel_id=1, source_target_pairs={{2,7},{3,6},{4,1},{5,0},{6,11},{7,10},{8,5},{9,4},{10,15},{11,14},... | collective-permute-start | bytes 897032 | tf_op jit(solution)/shard_map/ppermute | solution.py:463
  14.0 15.4 %collective-permute-start.1 = (f32[584,128]{1,0:T(8,128)S(1)}, f32[584,128]{1,0:T(8,128)S(1)}, u32[]{:S(2)}, u32[]{:S(2)}) collective-permute-start(f32[584,128]{1,0:T(8,128)S(1)} %collective-permute-done.refs_2_), channel_id=1, source_target_pairs={{0,4},{1,5},{4,8},{5,9},{6,2},{7,3},{8,12},{9,13},{10,6},{11,7},{1... | collective-permute-start | bytes 897032 | tf_op jit(solution)/shard_map/ppermute | solution.py:464
  18.8 10.8 %collective-permute-start.3 = (f32[584,128]{1,0:T(8,128)S(1)}, f32[584,128]{1,0:T(8,128)S(1)}, u32[]{:S(2)}, u32[]{:S(2)}) collective-permute-start(f32[584,128]{1,0:T(8,128)S(1)} %collective-permute-done.2.refs_3_), channel_id=1, source_target_pairs={{0,4},{1,5},{4,8},{5,9},{6,2},{7,3},{8,12},{9,13},{10,6},{11,7},{1... | collective-permute-start | bytes 897032 | tf_op jit(solution)/shard_map/ppermute | solution.py:464
  29.7 19.0 %copy-start.6 = (s32[1,2,128]{2,1,0:T(2,128)S(1)}, s32[1,2,128]{2,1,0:T(2,128)}, u32[]{:S(2)}) copy-start(s32[1,2,128]{2,1,0:T(2,128)} %param.7) | copy-start | bytes 3076
  33.2 13.6 %copy-start.1 = (f32[128,128]{1,0:T(8,128)}, f32[128,128]{1,0:T(8,128)S(1)}, u32[]{:S(2)}) copy-start(f32[128,128]{1,0:T(8,128)S(1)} %get-tuple-element.42.ray0) | copy-start | bytes 196612
  33.2 13.6 %copy-start.3 = (f32[128,128]{1,0:T(8,128)}, f32[128,128]{1,0:T(8,128)S(1)}, u32[]{:S(2)}) copy-start(f32[128,128]{1,0:T(8,128)S(1)} %get-tuple-element.43.coup0) | copy-start | bytes 196612
  33.2 13.6 %copy-start.5 = (f32[128,128]{1,0:T(8,128)}, f32[128,128]{1,0:T(8,128)S(1)}, u32[]{:S(2)}) copy-start(f32[128,128]{1,0:T(8,128)S(1)} %get-tuple-element.39) | copy-start | bytes 196612
  33.2 37.0 %collective-permute-start.14 = (f32[16,128,128]{2,1,0:T(8,128)S(1)}, f32[16,128,128]{2,1,0:T(8,128)S(1)}, u32[]{:S(2)}, u32[]{:S(2)}) collective-permute-start(f32[16,128,128]{2,1,0:T(8,128)S(1)} %get-tuple-element.34.refs_0_.out), channel_id=1, source_target_pairs={{0,16},{1,17},{2,18},{3,19},{4,20},{5,21},{6,22},{7,23},{8,24},{9,... | collective-permute-start | bytes 3145736 | tf_op jit(solution)/shard_map/ppermute | solution.py:545
  36.6 1.4 %collective-permute-start.10 = (f32[192,128]{1,0:T(8,128)S(1)}, f32[192,128]{1,0:T(8,128)S(1)}, u32[]{:S(2)}, u32[]{:S(2)}) collective-permute-start(f32[192,128]{1,0:T(8,128)S(1)} %get-tuple-element.38), channel_id=1, source_target_pairs={{0,1},{1,0},{2,3},{3,2},{4,5},{5,4},{6,7},{7,6},{8,9},{9,8},{10,11... | collective-permute-start | bytes 294920 | tf_op jit(solution)/shard_map/ppermute | solution.py:407
  38.0 7.1 %collective-permute-start.11 = (f32[192,128]{1,0:T(8,128)S(1)}, f32[192,128]{1,0:T(8,128)S(1)}, u32[]{:S(2)}, u32[]{:S(2)}) collective-permute-start(f32[192,128]{1,0:T(8,128)S(1)} %add.83), channel_id=1, source_target_pairs={{0,2},{1,3},{2,0},{3,1},{4,6},{5,7},{6,4},{7,5},{8,10},{9,11},{10,... | collective-permute-start | bytes 294920 | tf_op jit(solution)/shard_map/ppermute | solution.py:407
  45.1 4.8 %collective-permute-start.12 = (f32[192,128]{1,0:T(8,128)S(1)}, f32[192,128]{1,0:T(8,128)}, u32[]{:S(2)}, u32[]{:S(2)}) collective-permute-start(f32[192,128]{1,0:T(8,128)S(1)} %add.84), channel_id=1, source_target_pairs={{0,4},{1,5},{2,6},{3,7},{4,0},{5,1},{6,2},{7,3},{8,12},{9,13},{10,... | collective-permute-start | bytes 294920 | tf_op jit(solution)/shard_map/ppermute | solution.py:407
  46.7 23.4 %collective-permute-start.7 = (f32[528,128]{1,0:T(8,128)}, f32[528,128]{1,0:T(8,128)S(1)}, u32[]{:S(2)}, u32[]{:S(2)}) collective-permute-start(f32[528,128]{1,0:T(8,128)} %get-tuple-element.35), channel_id=1, source_target_pairs={{0,1},{1,0},{2,3},{3,2},{4,5},{5,4},{6,7},{7,6},{8,9},{9,8},{10,11... | collective-permute-start | bytes 811016 | tf_op jit(solution)/shard_map/ppermute | solution.py:407
  46.8 23.4 %collective-permute-start.9 = (f32[528,128]{1,0:T(8,128)S(1)}, f32[528,128]{1,0:T(8,128)S(1)}, u32[]{:S(2)}, u32[]{:S(2)}) collective-permute-start(f32[528,128]{1,0:T(8,128)S(1)} %get-tuple-element.37), channel_id=1, source_target_pairs={{0,3},{1,2},{2,1},{3,0},{4,7},{5,6},{6,5},{7,4},{8,11},{9,10},{10,... | collective-permute-start | bytes 811016 | tf_op jit(solution)/shard_map/ppermute | solution.py:407
  49.6 20.6 %copy-start.2 = (f32[128,128]{1,0:T(8,128)S(1)}, f32[128,128]{1,0:T(8,128)}, u32[]{:S(2)}) copy-start(f32[128,128]{1,0:T(8,128)} %copy-done.1) | copy-start | bytes 196612
  49.6 20.6 %copy-start.4 = (f32[128,128]{1,0:T(8,128)S(1)}, f32[128,128]{1,0:T(8,128)}, u32[]{:S(2)}) copy-start(f32[128,128]{1,0:T(8,128)} %copy-done.3) | copy-start | bytes 196612
  50.8 7.6 %collective-permute-start.13 = (f32[192,128]{1,0:T(8,128)S(1)}, f32[192,128]{1,0:T(8,128)S(1)}, u32[]{:S(2)}, u32[]{:S(2)}) collective-permute-start(f32[192,128]{1,0:T(8,128)S(1)} %add.85.packed), channel_id=1, source_target_pairs={{0,8},{1,9},{2,10},{3,11},{4,12},{5,13},{6,14},{7,15},{8,0},{9,1},... | collective-permute-start | bytes 294920 | tf_op jit(solution)/shard_map/ppermute | solution.py:407
  52.9 24.6 %collective-permute-start.8 = (f32[528,128]{1,0:T(8,128)S(1)}, f32[528,128]{1,0:T(8,128)}, u32[]{:S(2)}, u32[]{:S(2)}) collective-permute-start(f32[528,128]{1,0:T(8,128)S(1)} %get-tuple-element.36), channel_id=1, source_target_pairs={{0,2},{1,3},{2,0},{3,1},{4,6},{5,7},{6,4},{7,5},{8,10},{9,11},{10,... | collective-permute-start | bytes 811016 | tf_op jit(solution)/shard_map/ppermute | solution.py:407
  58.4 10.4 %collective-permute-start.15 = (f32[128,128]{1,0:T(8,128)}, f32[128,128]{1,0:T(8,128)S(1)}, u32[]{:S(2)}, u32[]{:S(2)}) collective-permute-start(f32[128,128]{1,0:T(8,128)} %copy-done.5), channel_id=1, source_target_pairs={{2,6},{3,7},{4,0},{5,1},{6,10},{7,11},{8,4},{9,5},{10,14},{11,15},... | collective-permute-start | bytes 196616 | tf_op jit(solution)/shard_map/ppermute | solution.py:547
  68.8 3.2 %collective-permute-start.16 = (f32[128,128]{1,0:T(8,128)S(1)}, f32[128,128]{1,0:T(8,128)S(1)}, u32[]{:S(2)}, u32[]{:S(2)}) collective-permute-start(f32[128,128]{1,0:T(8,128)S(1)} %mixing.1.refs_4_.mix), channel_id=1, source_target_pairs={{0,16},{1,17},{2,18},{3,19},{4,20},{5,21},{6,22},{7,23},{8,24},{9,... | collective-permute-start | bytes 196616 | tf_op jit(solution)/shard_map/ppermute | solution.py:578
  73.1 12.2 %all-to-all-start = ((f32[16,16,128]{2,1,0:T(8,128)}), f32[16,16,128]{2,1,0:T(8,128)S(1)}, u32[]{:S(2)}, u32[]{:S(2)}) async-start(f32[16,16,128]{2,1,0:T(8,128)} %bitcast.44), calls=%async_computation | async-start | bytes 262144 | tf_op jit(solution)/shard_map/all_to_all | solution.py:608
  (1 other events, 0.9 us)

commit v3 on v2

--- a/solution.py
+++ b/solution.py
@@ -387,7 +387,7 @@
 
     def place(value, at):
         for r in range(peers):
-            to = (2 * r + at) * share
+            to = (2 * ((r % 2) * (peers // 2) + r // 2) + at) * share
             shares[to : to + share, :] = value[r * share : (r + 1) * share, :]
 
     place(mm_t(mix[...], mm(ray[...] + ray[...].T, m)), 1)
@@ -604,8 +604,12 @@
         cost_estimate=pl.CostEstimate(flops=10**8, bytes_accessed=10**6, transcendentals=0),
         name="project",
     )(first, ray, coup, before, mix_now)
-    shares = shares.reshape(peers, 2 * share, nm)
-    shares = lax.all_to_all(shares, "rows", 0, 0).sum(0)
+    shares = shares.reshape(2, peers // 2, 2 * share, nm)
+    odd = (me & 1) == 1
+    there = xor_swap(jnp.where(odd, shares[0], shares[1]), "rows", 1)
+    shares = jnp.where(odd, shares[1], shares[0]) + there
+    sets = [list(range(bit, peers, 2)) for bit in range(2)]
+    shares = lax.all_to_all(shares, "rows", 0, 0, axis_index_groups=sets).sum(0)
     coupling, rayleigh = shares[:share], shares[share:]
 
     where = []

time: 86.4 us -> 86.6 us (level)
    ppermute x10 -> x11, waiting for transfers between devices: 14.5 us -> 15.7 us  [xor_swap(): return lax.ppermute(value, axis, [(i, i ^ bit) for i in range(peers)])]
    all_to_all x1, waiting for transfers between devices: 5.54 us -> 4.58 us  [body(): shares = lax.all_to_all(shares, 'rows', 0, 0, axis_index_groups=sets).sum(0)]
    ppermute x10 -> x11, starting transfers between devices: 14.2 us -> 14.3 us  [xor_swap(): return lax.ppermute(value, axis, [(i, i ^ bit) for i in range(peers)])]
  transfers between devices with their start and end apart: 18 -> 19, of which waited for: 10 -> 11; matrix products, arithmetic and copies ran while one was open for 2% -> 2% of each run, Pallas kernels for 23% -> 22%
where the time goes in v3:
time: 86.6 us; the launch traced here: 86.2 us
  starting transfers between devices  34.7 us (40%)
  Pallas kernels  22.4 us (26%)
  waiting for transfers between devices  22.2 us (26%)
  local copies, waits for them, and re-layouts  4.07 us (5%)
  other arithmetic  1.77 us (2%)
  between operations  1.08 us (1%)
    ppermute x11, waiting for transfers between devices, xor_swap(): return lax.ppermute(value, axis, [(i, i ^ bit) for i in range(peers)])  15.7 us
    ppermute x11, starting transfers between devices, xor_swap(): return lax.ppermute(value, axis, [(i, i ^ bit) for i in range(peers)])  14.3 us
    pallas_call x1, Pallas kernels, body(): pl.pallas_call(functools.partial(mixing_kernel, 1.0 / pixels), out_shape=...  8.87 us
    ppermute x2, starting transfers between devices, body(): lax.ppermute(arrived[k], 'rows', hop(0, True))  7.47 us
    pallas_call x1, Pallas kernels, body(): pl.pallas_call(functools.partial(near_kernel, dims), out_shape=(field_buf...  5.88 us
    all_to_all x1, waiting for transfers between devices, body(): shares = lax.all_to_all(shares, 'rows', 0, 0, axis_index_groups=sets).sum(0)  4.58 us
    all_to_all x1, starting transfers between devices, body(): shares = lax.all_to_all(shares, 'rows', 0, 0, axis_index_groups=sets).sum(0)  4.17 us
    pallas_call x1, Pallas kernels, body(): pl.pallas_call(functools.partial(far_kernel, dims), out_shape=(field_buff...  3.49 us
  transfers between devices with their start and end apart: 19, of which 11 were waited for; matrix products, arithmetic and copies ran while one was open for 2% of the time, Pallas kernels for 22%

profile of v3, /device:TPU:0, one launch (start us, length us, event | category | flops | bytes accessed | tf_op | source)
XLA Modules:
  0.0 86.2 jit_solution(5582323020288022828)
XLA Ops:
  1.6 1.4 %constant_dynamic-slice_fusion = (f32[1,4,144,128]{3,2,1,0:T(8,128)S(1)}, f32[1,4,144,128]{3,2,1,0:T(8,128)S(1)}, f32[1,4,144,128]{3,2,1,0:T(8,128)S(1)}, f32[1,4,144,128]{3,2,1,0:T(8,128)S(1)}) fusion(f32[1,4,512,128]{3,2,1,0:T(8,128)} %param.4, s32[]{:T(128)S(6)} %min.17, s32[]{:T(128)S(6)} %min.16, s32[]{:T(128)S(6)} %min.15, s32[]{:T(128)S(6)} %min.14), kind=kLoop, calls=%fused_computation.12 | loop fusion | bytes 2359312 | tf_op jit(solution)/shard_map/dynamic_slice | solution.py:449
  3.0 3.1 %collective-permute-start = (f32[584,128]{1,0:T(8,128)S(1)}, f32[584,128]{1,0:T(8,128)S(1)}, u32[]{:S(2)}, u32[]{:S(2)}) collective-permute-start(f32[584,128]{1,0:T(8,128)S(1)} %pad_maximum_fusion), channel_id=1, source_target_pairs={{0,2},{1,3},{2,0},{3,1},{4,6},{5,7},{6,4},{7,5},{8,10},{9,11},{10,... | collective-permute-start | bytes 897032 | tf_op jit(solution)/shard_map/ppermute | solution.py:407
  6.5 1.3 %collective-permute-start.5 = (f32[584,128]{1,0:T(8,128)S(1)}, f32[584,128]{1,0:T(8,128)S(1)}, u32[]{:S(2)}, u32[]{:S(2)}) collective-permute-start(f32[584,128]{1,0:T(8,128)S(1)} %pad_maximum_fusion.2.refs_0_), channel_id=1, source_target_pairs={{2,6},{3,7},{4,0},{5,1},{6,10},{7,11},{8,4},{9,5},{10,14},{11,15},... | collective-permute-start | bytes 897032 | tf_op jit(solution)/shard_map/ppermute | solution.py:463
  7.8 1.3 %collective-permute-start.6 = (f32[584,128]{1,0:T(8,128)S(1)}, f32[584,128]{1,0:T(8,128)S(1)}, u32[]{:S(2)}, u32[]{:S(2)}) collective-permute-start(f32[584,128]{1,0:T(8,128)S(1)} %pad_maximum_fusion.3), channel_id=1, source_target_pairs={{2,7},{3,6},{4,1},{5,0},{6,11},{7,10},{8,5},{9,4},{10,15},{11,14},... | collective-permute-start | bytes 897032 | tf_op jit(solution)/shard_map/ppermute | solution.py:463
  9.1 4.9 %collective-permute-done.refs_2_ = f32[584,128]{1,0:T(8,128)S(1)} collective-permute-done((f32[584,128]{1,0:T(8,128)S(1)}, f32[584,128]{1,0:T(8,128)S(1)}, u32[]{:S(2)}, u32[]{:S(2)}) %collective-permute-start) | collective-permute-done | bytes 299040 | tf_op jit(solution)/shard_map/ppermute | solution.py:407
  14.0 4.0 %collective-permute-start.1 = (f32[584,128]{1,0:T(8,128)S(1)}, f32[584,128]{1,0:T(8,128)S(1)}, u32[]{:S(2)}, u32[]{:S(2)}) collective-permute-start(f32[584,128]{1,0:T(8,128)S(1)} %collective-permute-done.refs_2_), channel_id=1, source_target_pairs={{0,4},{1,5},{4,8},{5,9},{6,2},{7,3},{8,12},{9,13},{10,6},{11,7},{1... | collective-permute-start | bytes 897032 | tf_op jit(solution)/shard_map/ppermute | solution.py:464
  18.8 3.5 %collective-permute-start.3 = (f32[584,128]{1,0:T(8,128)S(1)}, f32[584,128]{1,0:T(8,128)S(1)}, u32[]{:S(2)}, u32[]{:S(2)}) collective-permute-start(f32[584,128]{1,0:T(8,128)S(1)} %collective-permute-done.2.refs_3_), channel_id=1, source_target_pairs={{0,4},{1,5},{4,8},{5,9},{6,2},{7,3},{8,12},{9,13},{10,6},{11,7},{1... | collective-permute-start | bytes 897032 | tf_op jit(solution)/shard_map/ppermute | solution.py:464
  23.6 5.9 %near.1 = (f32[32,160,128]{2,1,0:T(8,128)S(1)}, f32[32,160,128]{2,1,0:T(8,128)S(1)}, f32[32,160,128]{2,1,0:T(8,128)S(1)}, f32[16,128,128]{2,1,0:T(8,128)S(1)}, f...) custom-call(s32[18]{0:T(128)S(1)} %stack.156.pos, ...), custom_call_target="tpu_custom_call" | custom-call | flops 1000000000 | bytes 40000000 | tf_op jit(solution)/shard_map/near/pallas_call | solution.py:506
  29.7 3.5 %far.1 = (f32[32,160,128]{2,1,0:T(8,128)S(1)}, f32[32,160,128]{2,1,0:T(8,128)S(1)}, f32[32,160,128]{2,1,0:T(8,128)S(1)}, f32[192,128]{1,0:T(8,128)S(1)}, f32[128...) custom-call(s32[18]{0:T(128)S(1)} %stack.156.pos, ...), custom_call_target="tpu_custom_call", output_to_operand_aliasing={{0}: (3, {}), {1}: (4, {}), {2}: (5, {})} | custom-call | flops 1000000000 | bytes 20000000 | tf_op jit(solution)/shard_map/far/pallas_call | solution.py:524
  33.2 3.4 %collective-permute-start.14 = (f32[16,128,128]{2,1,0:T(8,128)S(1)}, f32[16,128,128]{2,1,0:T(8,128)S(1)}, u32[]{:S(2)}, u32[]{:S(2)}) collective-permute-start(f32[16,128,128]{2,1,0:T(8,128)S(1)} %get-tuple-element.34.refs_0_.out), channel_id=1, source_target_pairs={{0,16},{1,17},{2,18},{3,19},{4,20},{5,21},{6,22},{7,23},{8,24},{9,... | collective-permute-start | bytes 3145736 | tf_op jit(solution)/shard_map/ppermute | solution.py:545
  36.8 1.2 %collective-permute-done.10 = f32[192,128]{1,0:T(8,128)S(1)} collective-permute-done((f32[192,128]{1,0:T(8,128)S(1)}, f32[192,128]{1,0:T(8,128)S(1)}, u32[]{:S(2)}, u32[]{:S(2)}) %collective-permute-start.10) | collective-permute-done | bytes 98336 | tf_op jit(solution)/shard_map/ppermute | solution.py:407
  38.0 4.0 %collective-permute-start.11 = (f32[192,128]{1,0:T(8,128)S(1)}, f32[192,128]{1,0:T(8,128)S(1)}, u32[]{:S(2)}, u32[]{:S(2)}) collective-permute-start(f32[192,128]{1,0:T(8,128)S(1)} %add.86), channel_id=1, source_target_pairs={{0,2},{1,3},{2,0},{3,1},{4,6},{5,7},{6,4},{7,5},{8,10},{9,11},{10,... | collective-permute-start | bytes 294920 | tf_op jit(solution)/shard_map/ppermute | solution.py:407
  42.0 3.1 %collective-permute-done.11 = f32[192,128]{1,0:T(8,128)S(1)} collective-permute-done((f32[192,128]{1,0:T(8,128)S(1)}, f32[192,128]{1,0:T(8,128)S(1)}, u32[]{:S(2)}, u32[]{:S(2)}) %collective-permute-start.11) | collective-permute-done | bytes 98336 | tf_op jit(solution)/shard_map/ppermute | solution.py:407
  45.1 1.6 %collective-permute-start.12 = (f32[192,128]{1,0:T(8,128)S(1)}, f32[192,128]{1,0:T(8,128)}, u32[]{:S(2)}, u32[]{:S(2)}) collective-permute-start(f32[192,128]{1,0:T(8,128)S(1)} %add.87), channel_id=1, source_target_pairs={{0,4},{1,5},{2,6},{3,7},{4,0},{5,1},{6,2},{7,3},{8,12},{9,13},{10,... | collective-permute-start | bytes 294920 | tf_op jit(solution)/shard_map/ppermute | solution.py:407
  46.8 1.9 %collective-permute-start.9 = (f32[528,128]{1,0:T(8,128)S(1)}, f32[528,128]{1,0:T(8,128)S(1)}, u32[]{:S(2)}, u32[]{:S(2)}) collective-permute-start(f32[528,128]{1,0:T(8,128)S(1)} %get-tuple-element.37), channel_id=1, source_target_pairs={{0,3},{1,2},{2,1},{3,0},{4,7},{5,6},{6,5},{7,4},{8,11},{9,10},{10,... | collective-permute-start | bytes 811016 | tf_op jit(solution)/shard_map/ppermute | solution.py:407
  50.8 2.1 %collective-permute-start.13 = (f32[192,128]{1,0:T(8,128)S(1)}, f32[192,128]{1,0:T(8,128)S(1)}, u32[]{:S(2)}, u32[]{:S(2)}) collective-permute-start(f32[192,128]{1,0:T(8,128)S(1)} %add.88.packed), channel_id=1, source_target_pairs={{0,8},{1,9},{2,10},{3,11},{4,12},{5,13},{6,14},{7,15},{8,0},{9,1},... | collective-permute-start | bytes 294920 | tf_op jit(solution)/shard_map/ppermute | solution.py:407
  54.1 4.4 %collective-permute-done.13.there = f32[192,128]{1,0:T(8,128)S(1)} collective-permute-done((f32[192,128]{1,0:T(8,128)S(1)}, f32[192,128]{1,0:T(8,128)S(1)}, u32[]{:S(2)}, u32[]{:S(2)}) %collective-permute-start.13) | collective-permute-done | bytes 98336 | tf_op jit(solution)/shard_map/ppermute | solution.py:407
  58.4 1.5 %collective-permute-start.15 = (f32[128,128]{1,0:T(8,128)}, f32[128,128]{1,0:T(8,128)S(1)}, u32[]{:S(2)}, u32[]{:S(2)}) collective-permute-start(f32[128,128]{1,0:T(8,128)} %copy-done.5), channel_id=1, source_target_pairs={{2,6},{3,7},{4,0},{5,1},{6,10},{7,11},{8,4},{9,5},{10,14},{11,15},... | collective-permute-start | bytes 196616 | tf_op jit(solution)/shard_map/ppermute | solution.py:547
  59.9 8.9 %mixing.1.refs_4_.mix = f32[128,128]{1,0:T(8,128)S(1)} custom-call(f32[192,128]{1,0:T(8,128)S(1)} %add.88.packed, f32[192,128]{1,0:T(8,128)S(1)} %collective-permute-done.13.there, f32[2,128,128]{2,1,0:T(8,128)S(1)} %turn.1.turned), custom_call_target="tpu_custom_call" | custom-call | flops 1000000000 | bytes 40000000 | tf_op jit(solution)/shard_map/mixing/pallas_call | solution.py:563
  68.8 1.3 %collective-permute-start.16 = (f32[128,128]{1,0:T(8,128)S(1)}, f32[128,128]{1,0:T(8,128)S(1)}, u32[]{:S(2)}, u32[]{:S(2)}) collective-permute-start(f32[128,128]{1,0:T(8,128)S(1)} %mixing.1.refs_4_.mix), channel_id=1, source_target_pairs={{0,16},{1,17},{2,18},{3,19},{4,20},{5,21},{6,22},{7,23},{8,24},{9,... | collective-permute-start | bytes 196616 | tf_op jit(solution)/shard_map/ppermute | solution.py:578
  72.6 1.2 %collective-permute-done.17 = f32[8,16,128]{2,1,0:T(8,128)S(1)} collective-permute-done((f32[8,16,128]{2,1,0:T(8,128)S(1)}, f32[8,16,128]{2,1,0:T(8,128)S(1)}, u32[]{:S(2)}, u32[]{:S(2)}) %collective-permute-start.17) | collective-permute-done | bytes 65568 | tf_op jit(solution)/shard_map/ppermute | solution.py:407
  74.5 4.2 %all-to-all-start = ((f32[8,16,128]{2,1,0:T(8,128)}), f32[8,16,128]{2,1,0:T(8,128)S(1)}, u32[]{:S(2)}, u32[]{:S(2)}) async-start(f32[8,16,128]{2,1,0:T(8,128)} %add.90), calls=%async_computation | async-start | bytes 131072 | tf_op jit(solution)/shard_map/all_to_all | solution.py:612
  78.7 2.2 %modes.1 = f32[4,512,128]{2,1,0:T(8,128)} custom-call(s32[12]{0:T(128)S(1)} %stack.135.pos, f32[16,128,128]{2,1,0:T(8,128)S(1)} %get-tuple-element.34.refs_0_.out, f32[528,128]{1,0:T(8,128)S(1)} %collective-permute-done.7.refs_1_.refs_0_, f32[528,128]{1,0:T(8,128)} %collective-permute-done.8.refs_2_, f32[528,128]{1,0:T(8,128)S(1)} %collective-permute-done.9.refs_3_.refs_1_, ...), custom_call_target="tpu_custom_call" | custom-call | flops 1000000000 | bytes 10000000 | tf_op jit(solution)/shard_map/modes/pallas_call | solution.py:628
  81.0 4.6 %all-to-all-done = f32[8,16,128]{2,1,0:T(8,128)S(1)} async-done(((f32[8,16,128]{2,1,0:T(8,128)}), f32[8,16,128]{2,1,0:T(8,128)S(1)}, u32[]{:S(2)}, u32[]{:S(2)}) %all-to-all-start) | async-done | bytes 65568 | tf_op jit(solution)/shard_map/all_to_all | solution.py:612
  (59 shorter events, 10.8 us)
Async XLA Ops:
  3.0 11.0 %collective-permute-start = (f32[584,128]{1,0:T(8,128)S(1)}, f32[584,128]{1,0:T(8,128)S(1)}, u32[]{:S(2)}, u32[]{:S(2)}) collective-permute-start(f32[584,128]{1,0:T(8,128)S(1)} %pad_maximum_fusion), channel_id=1, source_target_pairs={{0,2},{1,3},{2,0},{3,1},{4,6},{5,7},{6,4},{7,5},{8,10},{9,11},{10,... | collective-permute-start | bytes 897032 | tf_op jit(solution)/shard_map/ppermute | solution.py:407
  6.1 12.7 %collective-permute-start.2 = (f32[584,128]{1,0:T(8,128)S(1)}, f32[584,128]{1,0:T(8,128)S(1)}, u32[]{:S(2)}, u32[]{:S(2)}) collective-permute-start(f32[584,128]{1,0:T(8,128)S(1)} %pad_maximum_fusion.1), channel_id=1, source_target_pairs={{0,3},{1,2},{2,1},{3,0},{4,7},{5,6},{6,5},{7,4},{8,11},{9,10},{10,... | collective-permute-start | bytes 897032 | tf_op jit(solution)/shard_map/ppermute | solution.py:407
  6.3 16.3 %collective-permute-start.4 = (f32[584,128]{1,0:T(8,128)S(1)}, f32[584,128]{1,0:T(8,128)S(1)}, u32[]{:S(2)}, u32[]{:S(2)}) collective-permute-start(f32[584,128]{1,0:T(8,128)S(1)} %pad_maximum_fusion.3), channel_id=1, source_target_pairs={{0,1},{1,0},{2,3},{3,2},{4,5},{5,4},{6,7},{7,6},{8,9},{9,8},{10,11... | collective-permute-start | bytes 897032 | tf_op jit(solution)/shard_map/ppermute | solution.py:407
  6.5 16.1 %collective-permute-start.5 = (f32[584,128]{1,0:T(8,128)S(1)}, f32[584,128]{1,0:T(8,128)S(1)}, u32[]{:S(2)}, u32[]{:S(2)}) collective-permute-start(f32[584,128]{1,0:T(8,128)S(1)} %pad_maximum_fusion.2.refs_0_), channel_id=1, source_target_pairs={{2,6},{3,7},{4,0},{5,1},{6,10},{7,11},{8,4},{9,5},{10,14},{11,15},... | collective-permute-start | bytes 897032 | tf_op jit(solution)/shard_map/ppermute | solution.py:463
  7.8 15.8 %collective-permute-start.6 = (f32[584,128]{1,0:T(8,128)S(1)}, f32[584,128]{1,0:T(8,128)S(1)}, u32[]{:S(2)}, u32[]{:S(2)}) collective-permute-start(f32[584,128]{1,0:T(8,128)S(1)} %pad_maximum_fusion.3), channel_id=1, source_target_pairs={{2,7},{3,6},{4,1},{5,0},{6,11},{7,10},{8,5},{9,4},{10,15},{11,14},... | collective-permute-start | bytes 897032 | tf_op jit(solution)/shard_map/ppermute | solution.py:463
  14.0 15.4 %collective-permute-start.1 = (f32[584,128]{1,0:T(8,128)S(1)}, f32[584,128]{1,0:T(8,128)S(1)}, u32[]{:S(2)}, u32[]{:S(2)}) collective-permute-start(f32[584,128]{1,0:T(8,128)S(1)} %collective-permute-done.refs_2_), channel_id=1, source_target_pairs={{0,4},{1,5},{4,8},{5,9},{6,2},{7,3},{8,12},{9,13},{10,6},{11,7},{1... | collective-permute-start | bytes 897032 | tf_op jit(solution)/shard_map/ppermute | solution.py:464
  18.8 10.8 %collective-permute-start.3 = (f32[584,128]{1,0:T(8,128)S(1)}, f32[584,128]{1,0:T(8,128)S(1)}, u32[]{:S(2)}, u32[]{:S(2)}) collective-permute-start(f32[584,128]{1,0:T(8,128)S(1)} %collective-permute-done.2.refs_3_), channel_id=1, source_target_pairs={{0,4},{1,5},{4,8},{5,9},{6,2},{7,3},{8,12},{9,13},{10,6},{11,7},{1... | collective-permute-start | bytes 897032 | tf_op jit(solution)/shard_map/ppermute | solution.py:464
  29.7 19.0 %copy-start.6 = (s32[1,2,128]{2,1,0:T(2,128)S(1)}, s32[1,2,128]{2,1,0:T(2,128)}, u32[]{:S(2)}) copy-start(s32[1,2,128]{2,1,0:T(2,128)} %param.7) | copy-start | bytes 3076
  33.2 13.6 %copy-start.3 = (f32[128,128]{1,0:T(8,128)}, f32[128,128]{1,0:T(8,128)S(1)}, u32[]{:S(2)}) copy-start(f32[128,128]{1,0:T(8,128)S(1)} %get-tuple-element.43.coup0) | copy-start | bytes 196612
  33.2 13.6 %copy-start.5 = (f32[128,128]{1,0:T(8,128)}, f32[128,128]{1,0:T(8,128)S(1)}, u32[]{:S(2)}) copy-start(f32[128,128]{1,0:T(8,128)S(1)} %get-tuple-element.39) | copy-start | bytes 196612
  33.2 37.0 %collective-permute-start.14 = (f32[16,128,128]{2,1,0:T(8,128)S(1)}, f32[16,128,128]{2,1,0:T(8,128)S(1)}, u32[]{:S(2)}, u32[]{:S(2)}) collective-permute-start(f32[16,128,128]{2,1,0:T(8,128)S(1)} %get-tuple-element.34.refs_0_.out), channel_id=1, source_target_pairs={{0,16},{1,17},{2,18},{3,19},{4,20},{5,21},{6,22},{7,23},{8,24},{9,... | collective-permute-start | bytes 3145736 | tf_op jit(solution)/shard_map/ppermute | solution.py:545
  36.6 1.4 %collective-permute-start.10 = (f32[192,128]{1,0:T(8,128)S(1)}, f32[192,128]{1,0:T(8,128)S(1)}, u32[]{:S(2)}, u32[]{:S(2)}) collective-permute-start(f32[192,128]{1,0:T(8,128)S(1)} %get-tuple-element.38), channel_id=1, source_target_pairs={{0,1},{1,0},{2,3},{3,2},{4,5},{5,4},{6,7},{7,6},{8,9},{9,8},{10,11... | collective-permute-start | bytes 294920 | tf_op jit(solution)/shard_map/ppermute | solution.py:407
  38.0 7.1 %collective-permute-start.11 = (f32[192,128]{1,0:T(8,128)S(1)}, f32[192,128]{1,0:T(8,128)S(1)}, u32[]{:S(2)}, u32[]{:S(2)}) collective-permute-start(f32[192,128]{1,0:T(8,128)S(1)} %add.86), channel_id=1, source_target_pairs={{0,2},{1,3},{2,0},{3,1},{4,6},{5,7},{6,4},{7,5},{8,10},{9,11},{10,... | collective-permute-start | bytes 294920 | tf_op jit(solution)/shard_map/ppermute | solution.py:407
  45.1 4.8 %collective-permute-start.12 = (f32[192,128]{1,0:T(8,128)S(1)}, f32[192,128]{1,0:T(8,128)}, u32[]{:S(2)}, u32[]{:S(2)}) collective-permute-start(f32[192,128]{1,0:T(8,128)S(1)} %add.87), channel_id=1, source_target_pairs={{0,4},{1,5},{2,6},{3,7},{4,0},{5,1},{6,2},{7,3},{8,12},{9,13},{10,... | collective-permute-start | bytes 294920 | tf_op jit(solution)/shard_map/ppermute | solution.py:407
  46.7 23.4 %collective-permute-start.7 = (f32[528,128]{1,0:T(8,128)}, f32[528,128]{1,0:T(8,128)S(1)}, u32[]{:S(2)}, u32[]{:S(2)}) collective-permute-start(f32[528,128]{1,0:T(8,128)} %get-tuple-element.35), channel_id=1, source_target_pairs={{0,1},{1,0},{2,3},{3,2},{4,5},{5,4},{6,7},{7,6},{8,9},{9,8},{10,11... | collective-permute-start | bytes 811016 | tf_op jit(solution)/shard_map/ppermute | solution.py:407
  46.8 23.4 %collective-permute-start.9 = (f32[528,128]{1,0:T(8,128)S(1)}, f32[528,128]{1,0:T(8,128)S(1)}, u32[]{:S(2)}, u32[]{:S(2)}) collective-permute-start(f32[528,128]{1,0:T(8,128)S(1)} %get-tuple-element.37), channel_id=1, source_target_pairs={{0,3},{1,2},{2,1},{3,0},{4,7},{5,6},{6,5},{7,4},{8,11},{9,10},{10,... | collective-permute-start | bytes 811016 | tf_op jit(solution)/shard_map/ppermute | solution.py:407
  49.6 20.6 %copy-start.2 = (f32[128,128]{1,0:T(8,128)S(1)}, f32[128,128]{1,0:T(8,128)}, u32[]{:S(2)}) copy-start(f32[128,128]{1,0:T(8,128)} %copy-done.1) | copy-start | bytes 196612
  49.6 20.6 %copy-start.4 = (f32[128,128]{1,0:T(8,128)S(1)}, f32[128,128]{1,0:T(8,128)}, u32[]{:S(2)}) copy-start(f32[128,128]{1,0:T(8,128)} %copy-done.3) | copy-start | bytes 196612
  50.8 7.6 %collective-permute-start.13 = (f32[192,128]{1,0:T(8,128)S(1)}, f32[192,128]{1,0:T(8,128)S(1)}, u32[]{:S(2)}, u32[]{:S(2)}) collective-permute-start(f32[192,128]{1,0:T(8,128)S(1)} %add.88.packed), channel_id=1, source_target_pairs={{0,8},{1,9},{2,10},{3,11},{4,12},{5,13},{6,14},{7,15},{8,0},{9,1},... | collective-permute-start | bytes 294920 | tf_op jit(solution)/shard_map/ppermute | solution.py:407
  52.9 25.8 %collective-permute-start.8 = (f32[528,128]{1,0:T(8,128)S(1)}, f32[528,128]{1,0:T(8,128)}, u32[]{:S(2)}, u32[]{:S(2)}) collective-permute-start(f32[528,128]{1,0:T(8,128)S(1)} %get-tuple-element.36), channel_id=1, source_target_pairs={{0,2},{1,3},{2,0},{3,1},{4,6},{5,7},{6,4},{7,5},{8,10},{9,11},{10,... | collective-permute-start | bytes 811016 | tf_op jit(solution)/shard_map/ppermute | solution.py:407
  58.4 10.4 %collective-permute-start.15 = (f32[128,128]{1,0:T(8,128)}, f32[128,128]{1,0:T(8,128)S(1)}, u32[]{:S(2)}, u32[]{:S(2)}) collective-permute-start(f32[128,128]{1,0:T(8,128)} %copy-done.5), channel_id=1, source_target_pairs={{2,6},{3,7},{4,0},{5,1},{6,10},{7,11},{8,4},{9,5},{10,14},{11,15},... | collective-permute-start | bytes 196616 | tf_op jit(solution)/shard_map/ppermute | solution.py:547
  68.8 3.2 %collective-permute-start.16 = (f32[128,128]{1,0:T(8,128)S(1)}, f32[128,128]{1,0:T(8,128)S(1)}, u32[]{:S(2)}, u32[]{:S(2)}) collective-permute-start(f32[128,128]{1,0:T(8,128)S(1)} %mixing.1.refs_4_.mix), channel_id=1, source_target_pairs={{0,16},{1,17},{2,18},{3,19},{4,20},{5,21},{6,22},{7,23},{8,24},{9,... | collective-permute-start | bytes 196616 | tf_op jit(solution)/shard_map/ppermute | solution.py:578
  72.5 1.3 %collective-permute-start.17 = (f32[8,16,128]{2,1,0:T(8,128)S(1)}, f32[8,16,128]{2,1,0:T(8,128)S(1)}, u32[]{:S(2)}, u32[]{:S(2)}) collective-permute-start(f32[8,16,128]{2,1,0:T(8,128)S(1)} %bitcast.61), channel_id=1, source_target_pairs={{0,1},{1,0},{2,3},{3,2},{4,5},{5,4},{6,7},{7,6},{8,9},{9,8},{10,11... | collective-permute-start | bytes 196616 | tf_op jit(solution)/shard_map/ppermute | solution.py:407
  74.5 11.1 %all-to-all-start = ((f32[8,16,128]{2,1,0:T(8,128)}), f32[8,16,128]{2,1,0:T(8,128)S(1)}, u32[]{:S(2)}, u32[]{:S(2)}) async-start(f32[8,16,128]{2,1,0:T(8,128)} %add.90), calls=%async_computation | async-start | bytes 131072 | tf_op jit(solution)/shard_map/all_to_all | solution.py:612
  (2 other events, 14.5 us)
